TPU v7x, 256 devices: a whole 4x4x8 slice. The times are simulated.
256 devices in a mesh: sector: 128 (over z, y_lo, x, core), blk: 2 (over y_hi).
Axes of the slice: x: 4, y: 4 (y_hi: 2, y_lo: 2; y = y_hi * 2 + y_lo), z: 8, core: 2. Of those that a mesh axis runs over, the one named last changes fastest.
Arguments:
- signal: bfloat16 [4, 4096, 8192], P('blk', 'sector'), may hold values from -6 to 6
- offsets: int32 [4], P('blk'), may hold values from 0 to 4095
- fraction: float32 [4, 8192], P('blk'), may hold values from 0 to 1
- radius: float32 [256], replicated, may hold values from 0.2 to 0.9
- azimuth: float32 [256], replicated, may hold values from -3.140625 to 3.140625
Outputs:
- power: float32 [512, 256], P(('sector', 'blk'))
All inputs are finite; a program needn't handle non-finite values.
Results may differ from a plain program's by a relative error of at most 0.00095.
Values may be sent and summed in bfloat16 or wider, within the bound.
No kernel may reach another device: no remote copies, remote signals or barrier semaphores. Data moves between devices by JAX's collectives and lax.ppermute only.
A program may use at most 64 MiB of HBM per device.

v0:
```python
import math

import jax
import jax.numpy as jnp
from jax import lax
from jax.sharding import PartitionSpec as P

NFFT = 1024


wavenumber = 2.0
height = 0.5


def from_behind(x, axis, by):
    size = lax.axis_size(axis)
    return lax.ppermute(x, axis, [(i, (i + by) % size) for i in range(size)])


def fourier_table(groups):
    half_bins = NFFT // 2
    per_group = half_bins // groups
    sample = lax.iota(jnp.int32, NFFT)[:, None]
    column = lax.iota(jnp.int32, 2 * half_bins)[None, :]
    group = column // (2 * per_group)
    part = column // per_group % 2
    inner = column % per_group
    frequency = group * per_group + inner
    turns = (sample * frequency % NFFT).astype(jnp.float32)
    angle = turns * (2.0 * math.pi / NFFT)
    window = 0.5 - 0.5 * jnp.cos(sample.astype(jnp.float32) * (2.0 * math.pi / NFFT))
    value = jnp.where(part == 0, jnp.cos(angle), -jnp.sin(angle))
    return (value * window / math.sqrt(3.0 * NFFT / 8.0)).astype(jnp.bfloat16)


def distances(radius, azimuth, total_mics):
    turn = lax.iota(jnp.int32, total_mics).astype(jnp.float32) * (2.0 * math.pi / total_mics)
    cycle_cos = jnp.cos(turn)[:, None]
    cycle_sin = jnp.sin(turn)[:, None]
    across = (radius * jnp.cos(azimuth))[None, :]
    along = (radius * jnp.sin(azimuth))[None, :]
    squared = (
        1.0
        + height * height
        + (radius * radius)[None, :]
        - 2.0 * (cycle_cos * across + cycle_sin * along)
    )
    return jnp.sqrt(squared)


def steering(frequency, distance):
    phase = wavenumber * frequency.astype(jnp.float32) * distance
    return jnp.concatenate([jnp.cos(phase), jnp.sin(phase)], 1).astype(jnp.bfloat16)


def interpolate(window_rows, weight):
    lower = window_rows[:, :-1].astype(jnp.float32)
    upper = window_rows[:, 1:].astype(jnp.float32)
    spread_weight = weight[:, None, :]
    return ((1.0 - spread_weight) * lower + spread_weight * upper).astype(jnp.bfloat16)


def segment_spectra(virtual, table):
    blocks, mics, length = virtual.shape
    half = NFFT // 2
    halves = virtual.reshape(blocks, mics, length // half, half)
    upper = jnp.einsum(
        "bmhn,nc->bhcm", halves[:, :, :-1], table[:half], preferred_element_type=jnp.float32
    )
    lower = jnp.einsum(
        "bmhn,nc->bhcm", halves[:, :, 1:], table[half:], preferred_element_type=jnp.float32
    )
    return (upper + lower).astype(jnp.bfloat16)


def band_power(flat, first, count, distance):
    snapshots = flat.shape[0]
    points = distance.shape[1]

    def one_bin(bin_place):
        picked = lax.dynamic_index_in_dim(flat, bin_place, 2, keepdims=False)
        stacked = jnp.concatenate([picked[:, 0], picked[:, 1]], 0)
        steer = steering(first + bin_place, distance)
        product = jnp.dot(stacked, steer, preferred_element_type=jnp.float32)
        along = product[:snapshots, :points] + product[snapshots:, points:]
        across = product[snapshots:, :points] - product[:snapshots, points:]
        return jnp.sum(along * along + across * across, 0)

    return lax.map(one_bin, jnp.arange(count, dtype=jnp.int32))


def local(signal, offsets, fraction, radius, azimuth):
    blocks, mics, length = signal.shape
    sectors = lax.axis_size("sector")
    sector_index = lax.axis_index("sector")
    total_mics = mics * sectors
    hop_count = offsets // mics
    within = offsets % mics
    current = signal
    for place in range((sectors - 1).bit_length()):
        moved = from_behind(current, "sector", -(1 << place))
        chosen = hop_count // (1 << place) % 2 == 1
        current = jnp.where(chosen[:, None, None], moved, current)
    following = from_behind(current, "sector", -1)
    joined = jnp.concatenate([current, following], 1)
    window_rows = jax.vmap(lambda rows, start: lax.dynamic_slice_in_dim(rows, start, mics + 1, 0))(
        joined, within
    )
    virtual = interpolate(window_rows, fraction)
    spectra = segment_spectra(virtual, fourier_table(sectors))
    banded = lax.all_to_all(spectra, "sector", split_axis=2, concat_axis=3, tiled=True)
    segments = banded.shape[1]
    per_sector = banded.shape[2] // 2
    grouped = banded.reshape(blocks, segments, 2, per_sector, total_mics)
    distance = distances(radius, azimuth, total_mics)
    scale = 1.0 / (total_mics * blocks * segments * lax.axis_size("blk"))
    flat = grouped.reshape(blocks * segments, 2, per_sector, total_mics)
    partial_power = band_power(flat, sector_index * per_sector, per_sector, distance) * scale
    return lax.psum_scatter(partial_power, "blk", scatter_dimension=0, tiled=True)


def solution(mesh):
    return jax.shard_map(
        local,
        mesh=mesh,
        in_specs=(P("blk", "sector", None), P("blk"), P("blk", None), P(), P()),
        out_specs=P(("sector", "blk"), None),
        check_vma=False,
    )
```

profile of v0, /device:TPU:1, one launch (start us, length us, event | category | flops | bytes accessed | tf_op | source)
XLA Modules:
  0.0 480.9 jit_solution(11197837299432246893)
XLA Ops:
  3.9 11.4 %collective-permute-done = bf16[2,32,8192]{2,1,0:T(8,128)(2,1)S(1)} collective-permute-done((bf16[2,32,8192]{2,1,0:T(8,128)(2,1)}, bf16[2,32,8192]{2,1,0:T(8,128)(2,1)S(1)}, u32[]{:S(2)}, u32[]{:S(2)}) %collective-permute-start) | collective-permute-done | bytes 1048608 | tf_op jit(solution)/shard_map/ppermute | solution.py:17
  16.7 13.1 %collective-permute-start.1 = (bf16[2,32,8192]{2,1,0:T(8,128)(2,1)S(1)}, bf16[2,32,8192]{2,1,0:T(8,128)(2,1)S(1)}, u32[]{:S(2)}, u32[]{:S(2)}) collective-permute-start(bf16[2,32,8192]{2,1,0:T(8,128)(2,1)S(1)} %broadcast_select_fusion), channel_id=1, source_target_pairs={{0,252},{2,254},{4,0},{6,2},{8,4},{10,6},{12,8},{14,10},{16,12},{1... | collective-permute-start | bytes 3145736 | tf_op jit(solution)/shard_map/ppermute | solution.py:17
  29.8 18.4 %collective-permute-done.1 = bf16[2,32,8192]{2,1,0:T(8,128)(2,1)S(1)} collective-permute-done((bf16[2,32,8192]{2,1,0:T(8,128)(2,1)S(1)}, bf16[2,32,8192]{2,1,0:T(8,128)(2,1)S(1)}, u32[]{:S(2)}, u32[]{:S(2)}) %collective-permute-start.1) | collective-permute-done | bytes 1048608 | tf_op jit(solution)/shard_map/ppermute | solution.py:17
  50.3 21.5 %collective-permute-done.2 = bf16[2,32,8192]{2,1,0:T(8,128)(2,1)S(1)} collective-permute-done((bf16[2,32,8192]{2,1,0:T(8,128)(2,1)S(1)}, bf16[2,32,8192]{2,1,0:T(8,128)(2,1)S(1)}, u32[]{:S(2)}, u32[]{:S(2)}) %collective-permute-start.2) | collective-permute-done | bytes 1048608 | tf_op jit(solution)/shard_map/ppermute | solution.py:17
  74.4 21.9 %collective-permute-done.3 = bf16[2,32,8192]{2,1,0:T(8,128)(2,1)S(1)} collective-permute-done((bf16[2,32,8192]{2,1,0:T(8,128)(2,1)S(1)}, bf16[2,32,8192]{2,1,0:T(8,128)(2,1)S(1)}, u32[]{:S(2)}, u32[]{:S(2)}) %collective-permute-start.3) | collective-permute-done | bytes 1048608 | tf_op jit(solution)/shard_map/ppermute | solution.py:17
  100.0 21.4 %collective-permute-done.4 = bf16[2,32,8192]{2,1,0:T(8,128)(2,1)S(1)} collective-permute-done((bf16[2,32,8192]{2,1,0:T(8,128)(2,1)S(1)}, bf16[2,32,8192]{2,1,0:T(8,128)(2,1)S(1)}, u32[]{:S(2)}, u32[]{:S(2)}) %collective-permute-start.4) | collective-permute-done | bytes 1048608 | tf_op jit(solution)/shard_map/ppermute | solution.py:17
  124.4 37.4 %collective-permute-done.5 = bf16[2,32,8192]{2,1,0:T(8,128)(2,1)S(1)} collective-permute-done((bf16[2,32,8192]{2,1,0:T(8,128)(2,1)S(1)}, bf16[2,32,8192]{2,1,0:T(8,128)(2,1)S(1)}, u32[]{:S(2)}, u32[]{:S(2)}) %collective-permute-start.5) | collective-permute-done | bytes 1048608 | tf_op jit(solution)/shard_map/ppermute | solution.py:17
  164.7 45.3 %collective-permute-done.6 = bf16[2,32,8192]{2,1,0:T(8,128)(2,1)S(1)} collective-permute-done((bf16[2,32,8192]{2,1,0:T(8,128)(2,1)S(1)}, bf16[2,32,8192]{2,1,0:T(8,128)(2,1)S(1)}, u32[]{:S(2)}, u32[]{:S(2)}) %collective-permute-start.6) | collective-permute-done | bytes 1048608 | tf_op jit(solution)/shard_map/ppermute | solution.py:17
  214.9 18.0 %multiply_convert_fusion = bf16[1024,1024]{1,0:T(8,128)(2,1)} fusion(f32[1024]{0:T(1024)S(1)} %multiply_subtract_fusion, s32[1024]{0:T(1024)S(1)} %fusion.40, pred[1024]{0:T(1024)(128)(4,1)S(1)} %fusion.37), kind=kLoop, calls=%fused_computation.32 | loop fusion | flops 19922944 | bytes 2106368 | tf_op jit(solution)/shard_map/convert_element_type | solution.py:33
  234.3 5.4 %while.12 = (s32[]{:T(128)}, bf16[2,64,8192]{2,1,0:T(8,128)(2,1)S(1)}, s32[2,3]{1,0:T(2,128)S(1)}, bf16[2,33,8192]{2,1,0:T(8,128)(2,1)}, s32[]{:T(128)}) while((s32[]{:T(128)}, bf16[2,64,8192]{2,1,0:T(8,128)(2,1)S(1)}, s32[2,3]{1,0:T(2,128)S(1)}, bf16[2,33,8192]{2,1,0:T(8,128)(2,1)}, s32[]{:T(128)}) %tuple.63), condition=%wide.while_cond, body=%wide.while_body.sunk | while | flops 2 | bytes 1197673 | solution.py:106
  245.7 12.1 %copy.31 = bf16[2,15,1024,32]{3,0,1,2:T(2,128)(2,1)} copy(bf16[2,15,1024,32]{2,3,1,0:T(8,128)(2,1)S(1)} %fusion.24) | data formatting | bytes 3932160 | tf_op jit(solution)/shard_map/convert_element_type | solution.py:73
  257.8 16.9 %reshape.173 = bf16[128,2,3840]{2,1,0:T(2,128)(2,1)} reshape(bf16[1024,15,2,32]{3,2,1,0:T(2,128)(2,1)} %bitcast.50) | data formatting | bytes 3932160
  274.7 22.3 %all-to-all-start = ((bf16[128,2,3840]{2,1,0:T(2,128)(2,1)}), bf16[128,2,3840]{2,1,0:T(2,128)(2,1)S(1)}, u32[]{:S(2)}, u32[]{:S(2)}) async-start(bf16[128,2,3840]{2,1,0:T(2,128)(2,1)} %reshape.173), calls=%async_computation | async-start | bytes 3932160 | tf_op jit(solution)/shard_map/all_to_all | solution.py:111
  298.4 46.9 %all-to-all-done = bf16[128,2,3840]{2,1,0:T(2,128)(2,1)S(1)} async-done(((bf16[128,2,3840]{2,1,0:T(2,128)(2,1)}), bf16[128,2,3840]{2,1,0:T(2,128)(2,1)S(1)}, u32[]{:S(2)}, u32[]{:S(2)}) %all-to-all-start) | async-done | bytes 1966112 | tf_op jit(solution)/shard_map/all_to_all | solution.py:111
  345.4 6.6 %reshape.174 = bf16[1024,15,2,32]{3,2,1,0:T(2,128)(2,1)} reshape(bf16[128,2,3840]{2,1,0:T(2,128)(2,1)S(1)} %all-to-all-done) | data formatting | bytes 3932160
  352.0 5.0 %copy.49 = bf16[2,15,1024,32]{3,2,1,0:T(8,128)(2,1)S(1)} copy(bf16[2,15,1024,32]{3,0,1,2:T(2,128)(2,1)} %bitcast.51) | data formatting | bytes 3932160 | tf_op jit(solution)/shard_map/all_to_all | solution.py:111
  357.0 5.4 %copy.33 = bf16[2,15,8,128,32]{4,3,2,1,0:T(8,128)(2,1)} copy(bf16[2,15,8,128,32]{4,2,3,1,0:T(8,128)(2,1)S(1)} %bitcast.52) | data formatting | bytes 3932160 | tf_op jit(solution)/shard_map/all_to_all | solution.py:111
  362.4 11.3 %reshape_reshape.3 = bf16[30,2,4,4096]{3,2,1,0:T(4,128)(2,1)} reshape(bf16[2,15,8,128,32]{4,3,2,1,0:T(8,128)(2,1)} %copy.33) | data formatting | bytes 3932160 | tf_op jit(solution)/shard_map/reshape;reshape | solution.py:117
  377.4 97.6 %while.13 = (s32[]{:T(128)}, f32[4,256]{1,0:T(4,128)S(1)}, s32[4]{0:T(128)S(1)}, bf16[30,2,4,4096]{3,1,0,2:T(2,128)(2,1)S(1)}, s32[]{:T(128)}, /*index=5*/f32[25...) while((s32[]{:T(128)}, f32[4,256]{1,0:T(4,128)S(1)}, ...), condition=%wide.region_2.3_spmd.clone, body=%wide.region_0.2_spmd.clone.sunk | while | flops 269464320 | bytes 12114143 | solution.py:89
  382.6 18.4 %fusion.70 = (bf16[4096,256]{1,0:T(8,128)(2,1)S(1)}, bf16[4096,256]{1,0:T(8,128)(2,1)S(1)}) fusion(f32[256]{0:T(256)S(1)} %get-tuple-element.336, f32[4096]{0:T(1024)S(1)} %get-tuple-element.337, f32[256]{0:T(256)S(1)} %get-tuple-element.334, f32[4096]{0:T(1024)S(1)} %get-tuple-element.335, f32[256]{0:T(256)S(1)} %get-tuple-element.338, f32[]{:T(128)S(6)} %mul.373), kind=kLoop, calls=%fused_computation.10.clone.1 | loop fusion | flops 8388608 | bytes 4230148 | tf_op jit(solution)/shard_map/convert
  407.0 18.4 %fusion.70 = (bf16[4096,256]{1,0:T(8,128)(2,1)S(1)}, bf16[4096,256]{1,0:T(8,128)(2,1)S(1)}) fusion(f32[256]{0:T(256)S(1)} %get-tuple-element.336, f32[4096]{0:T(1024)S(1)} %get-tuple-element.337, f32[256]{0:T(256)S(1)} %get-tuple-element.334, f32[4096]{0:T(1024)S(1)} %get-tuple-element.335, f32[256]{0:T(256)S(1)} %get-tuple-element.338, f32[]{:T(128)S(6)} %mul.373), kind=kLoop, calls=%fused_computation.10.clone.1 | loop fusion | flops 8388608 | bytes 4230148 | tf_op jit(solution)/shard_map/convert
  431.4 18.4 %fusion.70 = (bf16[4096,256]{1,0:T(8,128)(2,1)S(1)}, bf16[4096,256]{1,0:T(8,128)(2,1)S(1)}) fusion(f32[256]{0:T(256)S(1)} %get-tuple-element.336, f32[4096]{0:T(1024)S(1)} %get-tuple-element.337, f32[256]{0:T(256)S(1)} %get-tuple-element.334, f32[4096]{0:T(1024)S(1)} %get-tuple-element.335, f32[256]{0:T(256)S(1)} %get-tuple-element.338, f32[]{:T(128)S(6)} %mul.373), kind=kLoop, calls=%fused_computation.10.clone.1 | loop fusion | flops 8388608 | bytes 4230148 | tf_op jit(solution)/shard_map/convert
  455.8 18.4 %fusion.70 = (bf16[4096,256]{1,0:T(8,128)(2,1)S(1)}, bf16[4096,256]{1,0:T(8,128)(2,1)S(1)}) fusion(f32[256]{0:T(256)S(1)} %get-tuple-element.336, f32[4096]{0:T(1024)S(1)} %get-tuple-element.337, f32[256]{0:T(256)S(1)} %get-tuple-element.334, f32[4096]{0:T(1024)S(1)} %get-tuple-element.335, f32[256]{0:T(256)S(1)} %get-tuple-element.338, f32[]{:T(128)S(6)} %mul.373), kind=kLoop, calls=%fused_computation.10.clone.1 | loop fusion | flops 8388608 | bytes 4230148 | tf_op jit(solution)/shard_map/convert
  475.0 5.3 %all-reduce.1 = f32[4,256]{1,0:T(4,128)S(1)} all-reduce(f32[4,256]{1,0:T(4,128)S(1)} %broadcast_multiply_fusion), channel_id=2, replica_groups=mesh['sector'=128,'blk'=2] {'blk'}, use_global_device_ids=true, to_apply=%region_3.4.clone | all-reduce | flops 1024 | bytes 8192
  (86 shorter events, 56.1 us)
Async XLA Ops:
  0.0 15.3 %collective-permute-start = (bf16[2,32,8192]{2,1,0:T(8,128)(2,1)}, bf16[2,32,8192]{2,1,0:T(8,128)(2,1)S(1)}, u32[]{:S(2)}, u32[]{:S(2)}) collective-permute-start(bf16[2,32,8192]{2,1,0:T(8,128)(2,1)} %param.7), channel_id=1, source_target_pairs={{0,254},{2,0},{4,2},{6,4},{8,6},{10,8},{12,10},{14,12},{16,14},{18... | collective-permute-start | bytes 3145736 | tf_op jit(solution)/shard_map/ppermute | solution.py:17
  16.7 31.4 %collective-permute-start.1 = (bf16[2,32,8192]{2,1,0:T(8,128)(2,1)S(1)}, bf16[2,32,8192]{2,1,0:T(8,128)(2,1)S(1)}, u32[]{:S(2)}, u32[]{:S(2)}) collective-permute-start(bf16[2,32,8192]{2,1,0:T(8,128)(2,1)S(1)} %broadcast_select_fusion), channel_id=1, source_target_pairs={{0,252},{2,254},{4,0},{6,2},{8,4},{10,6},{12,8},{14,10},{16,12},{1... | collective-permute-start | bytes 3145736 | tf_op jit(solution)/shard_map/ppermute | solution.py:17
  48.3 23.5 %collective-permute-start.2 = (bf16[2,32,8192]{2,1,0:T(8,128)(2,1)S(1)}, bf16[2,32,8192]{2,1,0:T(8,128)(2,1)S(1)}, u32[]{:S(2)}, u32[]{:S(2)}) collective-permute-start(bf16[2,32,8192]{2,1,0:T(8,128)(2,1)S(1)} %broadcast_select_fusion.1), channel_id=1, source_target_pairs={{0,248},{2,250},{4,252},{6,254},{8,0},{10,2},{12,4},{14,6},{16,8},... | collective-permute-start | bytes 3145736 | tf_op jit(solution)/shard_map/ppermute | solution.py:17
  71.8 52.6 %copy-start.3 = (s32[2]{0:T(128)S(1)}, s32[2]{0:T(128)}, u32[]{:S(2)}) copy-start(s32[2]{0:T(128)} %param.8) | copy-start | bytes 28
  72.0 24.3 %collective-permute-start.3 = (bf16[2,32,8192]{2,1,0:T(8,128)(2,1)S(1)}, bf16[2,32,8192]{2,1,0:T(8,128)(2,1)S(1)}, u32[]{:S(2)}, u32[]{:S(2)}) collective-permute-start(bf16[2,32,8192]{2,1,0:T(8,128)(2,1)S(1)} %broadcast_select_fusion.2), channel_id=1, source_target_pairs={{0,240},{2,242},{4,244},{6,246},{8,248},{10,250},{12,252},{14,254}... | collective-permute-start | bytes 3145736 | tf_op jit(solution)/shard_map/ppermute | solution.py:17
  96.3 68.4 %copy-start = (f32[2,8192]{1,0:T(2,128)S(1)}, f32[2,8192]{1,0:T(2,128)}, u32[]{:S(2)}) copy-start(f32[2,8192]{1,0:T(2,128)} %param.9) | copy-start | bytes 196612
  96.5 25.0 %collective-permute-start.4 = (bf16[2,32,8192]{2,1,0:T(8,128)(2,1)S(1)}, bf16[2,32,8192]{2,1,0:T(8,128)(2,1)S(1)}, u32[]{:S(2)}, u32[]{:S(2)}) collective-permute-start(bf16[2,32,8192]{2,1,0:T(8,128)(2,1)S(1)} %broadcast_select_fusion.3), channel_id=1, source_target_pairs={{0,224},{2,226},{4,228},{6,230},{8,232},{10,234},{12,236},{14,238}... | collective-permute-start | bytes 3145736 | tf_op jit(solution)/shard_map/ppermute | solution.py:17
  121.7 40.2 %collective-permute-start.5 = (bf16[2,32,8192]{2,1,0:T(8,128)(2,1)S(1)}, bf16[2,32,8192]{2,1,0:T(8,128)(2,1)S(1)}, u32[]{:S(2)}, u32[]{:S(2)}) collective-permute-start(bf16[2,32,8192]{2,1,0:T(8,128)(2,1)S(1)} %broadcast_select_fusion.4), channel_id=1, source_target_pairs={{0,192},{2,194},{4,196},{6,198},{8,200},{10,202},{12,204},{14,206}... | collective-permute-start | bytes 3145736 | tf_op jit(solution)/shard_map/ppermute | solution.py:17
  162.0 48.0 %collective-permute-start.6 = (bf16[2,32,8192]{2,1,0:T(8,128)(2,1)S(1)}, bf16[2,32,8192]{2,1,0:T(8,128)(2,1)S(1)}, u32[]{:S(2)}, u32[]{:S(2)}) collective-permute-start(bf16[2,32,8192]{2,1,0:T(8,128)(2,1)S(1)} %broadcast_select_fusion.5), channel_id=1, source_target_pairs={{0,128},{2,130},{4,132},{6,134},{8,136},{10,138},{12,140},{14,142}... | collective-permute-start | bytes 3145736 | tf_op jit(solution)/shard_map/ppermute | solution.py:17
  210.2 22.8 %collective-permute-start.7 = (bf16[2,32,8192]{2,1,0:T(8,128)(2,1)S(1)}, bf16[2,32,8192]{2,1,0:T(8,128)(2,1)}, u32[]{:S(2)}, u32[]{:S(2)}) collective-permute-start(bf16[2,32,8192]{2,1,0:T(8,128)(2,1)S(1)} %broadcast_select_fusion.6), channel_id=1, source_target_pairs={{0,254},{2,0},{4,2},{6,4},{8,6},{10,8},{12,10},{14,12},{16,14},{18... | collective-permute-start | bytes 3145736 | tf_op jit(solution)/shard_map/ppermute | solution.py:17
  239.7 3.2 copy-start.5
  257.8 39.2 %copy-start.4 = (u32[256]{0:T(256)S(1)}, u32[256]{0:T(256)}, u32[]{:S(2)}) copy-start(u32[256]{0:T(256)} %constant.255) | copy-start | bytes 3076
  257.8 40.5 %copy-start.1 = (f32[256]{0:T(256)S(1)}, f32[256]{0:T(256)}, u32[]{:S(2)}) copy-start(f32[256]{0:T(256)} %param.10) | copy-start | bytes 3076
  257.8 40.6 %copy-start.2 = (f32[256]{0:T(256)S(1)}, f32[256]{0:T(256)}, u32[]{:S(2)}) copy-start(f32[256]{0:T(256)} %param.11) | copy-start | bytes 3076
  274.7 70.7 %all-to-all-start = ((bf16[128,2,3840]{2,1,0:T(2,128)(2,1)}), bf16[128,2,3840]{2,1,0:T(2,128)(2,1)S(1)}, u32[]{:S(2)}, u32[]{:S(2)}) async-start(bf16[128,2,3840]{2,1,0:T(2,128)(2,1)} %reshape.173), calls=%async_computation | async-start | bytes 3932160 | tf_op jit(solution)/shard_map/all_to_all | solution.py:111
where the time goes:
time: 482 us; the launch traced here: 481 us
  waiting for transfers between devices  224 us (46%)
  other arithmetic  98.7 us (20%)
  local copies, waits for them, and re-layouts  79.3 us (16%)
  starting transfers between devices  56.5 us (12%)
  loops' own time  10.3 us (2%)
  matrix products  5.78 us (1%)
  blocking collectives  5.29 us (1%)
    ppermute x8, waiting for transfers between devices, from_behind(): return lax.ppermute(x, axis, [(i, (i + by) % size) for i in range(size)])  177 us
    another operation x4, other arithmetic  73.4 us
    all_to_all x1, waiting for transfers between devices, local(): lax.all_to_all(spectra, 'sector', split_axis=2, concat_axis=3, tiled=True)  46.9 us
    ppermute x8, starting transfers between devices, from_behind(): return lax.ppermute(x, axis, [(i, (i + by) % size) for i in range(size)])  34.2 us
    unnamed x20, local copies, waits for them, and re-layouts  28.7 us
    all_to_all x1, starting transfers between devices, local(): lax.all_to_all(spectra, 'sector', split_axis=2, concat_axis=3, tiled=True)  22.3 us
    convert_element_type x1, other arithmetic, fourier_table(): return (value * window / math.sqrt(3.0 * NFFT / 8.0)).astype(jnp.bfloat16)  18 us
    convert_element_type x1, local copies, waits for them, and re-layouts, segment_spectra(): return (upper + lower).astype(jnp.bfloat16)  12.1 us
  transfers between devices with their start and end apart: 9, of which 8 were waited for; matrix products, arithmetic and copies ran while one was open for 4% of the time, Pallas kernels for 0%

commit v1 on v0

v1 whole, which is shorter than its diff:
```python
import math

import jax
import jax.numpy as jnp
import numpy as np
from jax import lax
from jax.experimental import pallas as pl
from jax.experimental.pallas import tpu as pltpu
from jax.sharding import PartitionSpec as P

NFFT = 1024
HALF = NFFT // 2
LANES = 128
GROUP = 8

wavenumber = 2.0
height = 0.5

f32 = jnp.float32
bf16 = jnp.bfloat16


def fourier_tables(owners):
    sample = np.arange(NFFT)[None, :]
    per_owner = HALF // owners
    inner = np.arange(per_owner)[:, None, None]
    part = np.arange(2)[None, :, None]
    owner = np.arange(owners)[None, None, :]
    frequency = (owner * per_owner + inner + 0 * part).reshape(-1, 1)
    kind = (0 * owner + 0 * inner + part).reshape(-1, 1)
    angle = (sample * frequency % NFFT) * (2.0 * math.pi / NFFT)
    window = 0.5 - 0.5 * np.cos(sample * (2.0 * math.pi / NFFT))
    value = np.where(kind == 0, np.cos(angle), -np.sin(angle)) * window / math.sqrt(3.0 * NFFT / 8.0)
    value = value.astype(np.float32).astype(bf16)
    return value[:, :HALF], value[:, HALF:]


def spectra_body(offsets_ref, signal_ref, fraction_ref, upper_ref, lower_ref, out_ref, up_ref, low_ref, wide_ref):
    blocks, mics, length = signal_ref.shape
    halves = length // HALF
    owners = out_ref.shape[0]
    slot = blocks * halves
    rows = GROUP * slot
    lane = lax.broadcasted_iota(jnp.int32, (1, LANES), 1)
    row8 = lax.broadcasted_iota(jnp.int32, (GROUP, 1), 0)
    for group in range(mics // GROUP):
        base = group * GROUP
        for b in range(blocks):
            for h in range(halves):
                place = pl.ds(b * halves + h, GROUP, stride=slot)
                for q in range(HALF // LANES):
                    cols = slice(h * HALF + q * LANES, h * HALF + (q + 1) * LANES)
                    weight = fraction_ref[b : b + 1, cols]
                    here = signal_ref[b, base : base + GROUP, cols].astype(f32)
                    shifted = pltpu.roll(here, GROUP - 1, 0)
                    if base + GROUP < mics:
                        after = signal_ref[b, base + GROUP : base + GROUP + 1, cols].astype(f32)
                    else:
                        after = jnp.zeros((1, LANES), f32)
                    following = jnp.where(row8 == GROUP - 1, after, shifted)
                    mixed = (1.0 - weight) * here + weight * following
                    if h < halves - 1:
                        up_ref[q, place, :] = mixed
                    if h > 0:
                        low_ref[q, place, :] = mixed
        for m in range(GROUP):
            segment = base + m
            for b in range(blocks):
                top = m * slot + b * halves + halves - 1
                bottom = (top + 1) % rows
                if segment < halves - 1:
                    for ref, place, h in ((up_ref, top, segment), (low_ref, bottom, segment + 1)):
                        for q in range(HALF // LANES):
                            cols = slice(h * HALF + q * LANES, h * HALF + (q + 1) * LANES)
                            first = signal_ref[b, 0:1, cols].astype(f32)
                            ref[q, place : place + 1, :] = fraction_ref[b : b + 1, cols] * first
                else:
                    for q in range(HALF // LANES):
                        up_ref[q, top : top + 1, :] = jnp.zeros((1, LANES), f32)
                        low_ref[q, bottom : bottom + 1, :] = jnp.zeros((1, LANES), f32)
        contract = (((1,), (1,)), ((), ()))
        samples_up = jnp.concatenate([up_ref[q].astype(bf16) for q in range(HALF // LANES)], 1)
        samples_low = jnp.concatenate([low_ref[q].astype(bf16) for q in range(HALF // LANES)], 1)
        upper = lax.dot_general(upper_ref[...], samples_up, contract, preferred_element_type=f32)
        lower = lax.dot_general(lower_ref[...], samples_low, contract, preferred_element_type=f32)
        total = upper + pltpu.roll(lower, rows - 1, 1)
        for tile in range(rows // LANES):
            part = [total[c * owners : (c + 1) * owners, tile * LANES : (tile + 1) * LANES] for c in range(4)]
            for bit in (0, 1):
                step = slot << bit
                odd = (lane // step) % 2 == 1
                for c in range(4):
                    if c >> bit & 1 == 0:
                        a, z = part[c], part[c | 1 << bit]
                        part[c] = jnp.where(odd, pltpu.roll(z, step, 1), a)
                        part[c | 1 << bit] = jnp.where(odd, z, pltpu.roll(a, LANES - step, 1))
            for r in range(4):
                m = base + tile * 4 + r
                value = part[r]
                if m in (halves, halves + 1):
                    numbers = []
                    for b in range(blocks):
                        offset = offsets_ref[b]
                        numbers.append((offset // mics if m == halves else offset % mics).astype(f32))
                    note = jnp.where(lane // halves % 2 == 0, numbers[0], numbers[1])
                    value = jnp.where(lane % halves == halves - 1, note, value)
                wide_ref[pl.ds(m, owners, stride=mics), :] = value
    for owner in range(0, owners, 32):
        piece = wide_ref[owner * mics : (owner + 32) * mics, :]
        out_ref[owner : owner + 32] = piece.astype(bf16).reshape(32, mics, LANES)


def local_spectra(signal, offsets, fraction, owners):
    blocks, mics, length = signal.shape
    rows = GROUP * blocks * (length // HALF)
    upper, lower = fourier_tables(owners)
    vmem = pl.BlockSpec(memory_space=pltpu.VMEM)
    return pl.pallas_call(
        spectra_body,
        out_shape=jax.ShapeDtypeStruct((owners, mics, LANES), bf16),
        in_specs=[pl.BlockSpec(memory_space=pltpu.SMEM), vmem, vmem, vmem, vmem],
        out_specs=vmem,
        scratch_shapes=[
            pltpu.VMEM((HALF // LANES, rows, LANES), f32),
            pltpu.VMEM((HALF // LANES, rows, LANES), f32),
            pltpu.VMEM((owners * mics, LANES), f32),
        ],
        name="spectra",
    )(offsets, signal, fraction, jnp.asarray(upper), jnp.asarray(lower))


def cos_sin(phase):
    turns = jnp.round(phase * (1.0 / math.pi))
    rest = phase - turns * 3.140625
    rest = rest - turns * 9.67502593994140625e-4
    rest = rest - turns * 1.509957990978376432e-7
    half = turns * 0.5
    sign = 1.0 - 4.0 * (half - jnp.floor(half))
    square = rest * rest
    cosine = 1.0 / math.factorial(12)
    for order in (10, 8, 6, 4, 2, 0):
        cosine = cosine * square + (-1.0) ** (order // 2) / math.factorial(order)
    sine = -1.0 / math.factorial(11)
    for order in (9, 7, 5, 3, 1):
        sine = sine * square + (-1.0) ** (order // 2) / math.factorial(order)
    return sign * cosine, sign * rest * sine


STEER_COLS = 512


def steer_body(first_ref, cycle_ref, base_ref, across_ref, along_ref, out_ref):
    points = base_ref.shape[0]
    bins = out_ref.shape[0] // (2 * points)
    first = first_ref[0]
    cycle_cos = cycle_ref[0:1, :]
    cycle_sin = cycle_ref[1:2, :]

    def rows16(i, _):
        rows = pl.ds(pl.multiple_of(i * 16, 16), 16)
        squared = base_ref[rows, :] - 2.0 * (cycle_cos * across_ref[rows, :] + cycle_sin * along_ref[rows, :])
        distance = jnp.sqrt(squared)
        for j in range(bins):
            phase = wavenumber * (first + j).astype(f32) * distance
            cosine, sine = cos_sin(phase)
            place = pl.multiple_of(2 * j * points + i * 16, 16)
            out_ref[pl.ds(place, 16), :] = cosine.astype(bf16)
            place = pl.multiple_of((2 * j + 1) * points + i * 16, 16)
            out_ref[pl.ds(place, 16), :] = sine.astype(bf16)
        return 0

    lax.fori_loop(0, points // 16, rows16, 0)


def steering(first, bins, radius, azimuth, total_mics):
    turn = lax.iota(jnp.int32, total_mics).astype(f32) * (2.0 * math.pi / total_mics)
    cycle = jnp.stack([jnp.cos(turn), jnp.sin(turn)])
    points = radius.shape[0]
    base = (1.0 + height * height + radius * radius)[:, None]
    across = (radius * jnp.cos(azimuth))[:, None]
    along = (radius * jnp.sin(azimuth))[:, None]
    column = pl.BlockSpec((points, 1), lambda i: (0, 0))
    return pl.pallas_call(
        steer_body,
        grid=(total_mics // STEER_COLS,),
        out_shape=jax.ShapeDtypeStruct((bins * 2 * points, total_mics), bf16),
        in_specs=[
            pl.BlockSpec(memory_space=pltpu.SMEM),
            pl.BlockSpec((2, STEER_COLS), lambda i: (0, i)),
            column,
            column,
            column,
        ],
        out_specs=pl.BlockSpec((bins * 2 * points, STEER_COLS), lambda i: (0, i)),
        name="steer",
    )(first.reshape(1), cycle, base, across, along)


BEAM_ROWS = 512


def beam_body(received_ref, steer_ref, out_ref, wide_ref, start_ref, sum_ref, *, mics, blocks, halves, scale):
    step = pl.program_id(0)
    sources, groups = received_ref.shape[0], received_ref.shape[1]
    total = sources * mics
    lane = lax.broadcasted_iota(jnp.int32, (1, LANES), 1)
    spare = lane % halves == halves - 1
    of_block = lane // halves % blocks

    @pl.when(step == 0)
    def _():
        for group in range(groups):
            for source in range(0, sources, 16):
                piece = received_ref[source : source + 16, group].astype(f32).reshape(16 * mics, LANES)
                wide_ref[group, source * mics : (source + 16) * mics, :] = piece
            head = wide_ref[group, 0:mics, :]
            which = lax.broadcasted_iota(jnp.int32, (mics, LANES), 0)
            for b in range(blocks):
                mine = spare & (of_block == b) & (lane // (blocks * halves) == 0)
                hop = jnp.sum(jnp.where(mine & (which == halves), head, 0.0))
                within = jnp.sum(jnp.where(mine & (which == halves + 1), head, 0.0))
                start_ref[group * blocks + b] = hop.astype(jnp.int32) * mics + within.astype(jnp.int32)
            carried = jnp.zeros((sources, LANES), f32)
            for segment in range(halves - 1):
                rows = wide_ref[group, pl.ds(segment, sources, stride=mics), :]
                moved = pltpu.roll(jnp.where(spare, rows, 0.0), LANES - (halves - 1 - segment), 1)
                carried = carried + moved
            carried = pltpu.roll(carried, sources - 1, 0)
            last = pl.ds(mics - 1, sources, stride=mics)
            whole = wide_ref[group, last, :] + carried
            wide_ref[group, last, :] = whole
            wide_ref[group, total : total + BEAM_ROWS, :] = wide_ref[group, 0:BEAM_ROWS, :]
        sum_ref[...] = jnp.zeros(sum_ref.shape, f32)

    pieces = []
    for group in range(groups):
        start = [(start_ref[group * blocks + b] + step * BEAM_ROWS) % total for b in range(blocks)]
        rows = [wide_ref[group, pl.ds(s, BEAM_ROWS), :] for s in start]
        pieces.append(jnp.where(of_block == 0, rows[0], rows[1]).astype(bf16))
    stacked = jnp.concatenate(pieces, 1)
    sum_ref[...] += jnp.dot(steer_ref[...], stacked, preferred_element_type=f32)

    @pl.when(step == pl.num_programs(0) - 1)
    def _():
        points = out_ref.shape[1]
        slot = blocks * halves
        imaginary = lane // slot % 2 == 1
        for j in range(out_ref.shape[0]):
            power = jnp.zeros((points, LANES), f32)
            for group in range(groups):
                cols = slice(group * LANES, (group + 1) * LANES)
                by_cos = sum_ref[2 * j * points : (2 * j + 1) * points, cols]
                by_sin = sum_ref[(2 * j + 1) * points : (2 * j + 2) * points, cols]
                other = jnp.where(imaginary, -pltpu.roll(by_sin, slot, 1), pltpu.roll(by_sin, LANES - slot, 1))
                both = by_cos + other
                power = power + both * both
            power = jnp.where(~spare & (lane // (2 * slot) == j), power, 0.0)
            out_ref[j : j + 1, :] = jnp.sum(power.T, 0, keepdims=True) * scale


def beam(received, steer, mics, blocks, halves, points, scale):
    sources, groups = received.shape[:2]
    total = sources * mics
    bins = steer.shape[0] // (2 * points)
    body = lambda *refs: beam_body(*refs, mics=mics, blocks=blocks, halves=halves, scale=scale)
    return pl.pallas_call(
        body,
        grid=(total // BEAM_ROWS,),
        out_shape=jax.ShapeDtypeStruct((bins, points), f32),
        in_specs=[
            pl.BlockSpec(received.shape, lambda i: (0, 0, 0, 0)),
            pl.BlockSpec((steer.shape[0], BEAM_ROWS), lambda i: (0, i)),
        ],
        out_specs=pl.BlockSpec((bins, points), lambda i: (0, 0)),
        scratch_shapes=[
            pltpu.VMEM((groups, total + BEAM_ROWS, LANES), f32),
            pltpu.SMEM((groups * blocks,), jnp.int32),
            pltpu.VMEM((steer.shape[0], groups * LANES), f32),
        ],
        name="beam",
    )(received, steer)


def local(signal, offsets, fraction, radius, azimuth):
    blocks, mics, length = signal.shape
    sectors, groups = lax.axis_size("sector"), lax.axis_size("blk")
    owners = sectors * groups
    halves = length // HALF
    bins = HALF // owners
    spectra = local_spectra(signal, offsets, fraction, owners)
    moved = lax.all_to_all(spectra, ("sector", "blk"), split_axis=0, concat_axis=0, tiled=True)
    received = moved.reshape(sectors, groups, mics, LANES)
    first = (lax.axis_index("sector") * groups + lax.axis_index("blk")) * bins
    total_mics = sectors * mics
    steer = steering(first, bins, radius, azimuth, total_mics)
    scale = 1.0 / (total_mics * blocks * (halves - 1) * groups)
    return beam(received, steer, mics, blocks, halves, radius.shape[0], scale)


def solution(mesh):
    return jax.shard_map(
        local,
        mesh=mesh,
        in_specs=(P("blk", "sector", None), P("blk"), P("blk", None), P(), P()),
        out_specs=P(("sector", "blk"), None),
        check_vma=False,
    )
```

time: 482 us -> 97.2 us (0.20)
  waiting for transfers between devices: 224 us -> 25.9 us
  other arithmetic: 98.7 us -> 1.17 us
  local copies, waits for them, and re-layouts: 79.3 us -> 3.77 us
  Pallas kernels: 0 us -> 50.3 us
  starting transfers between devices: 56.5 us -> 15.7 us
  loops' own time: 10.3 us -> 0 us
  matrix products: 5.78 us -> 0 us
  blocking collectives: 5.29 us -> 0 us
    ppermute x8 -> x0, waiting for transfers between devices: 177 us -> none  [from_behind(): return lax.ppermute(x, axis, [(i, (i + by) % size) for i in range(size)])]
    another operation x4 -> x1, other arithmetic: 73.4 us -> 0.65 us  [steering(): cycle = jnp.stack([jnp.cos(turn), jnp.sin(turn)])]
    pallas_call x0 -> x3, Pallas kernels: none -> 50.3 us  [the longest x1 24.5 us: steering(): pl.pallas_call(steer_body, grid=(total_mics // STEER_COLS,), out_shape=ja...]
    ppermute x8 -> x0, starting transfers between devices: 34.2 us -> none  [from_behind(): return lax.ppermute(x, axis, [(i, (i + by) % size) for i in range(size)])]
    unnamed x20 -> x6, local copies, waits for them, and re-layouts: 28.7 us -> 1.37 us
    all_to_all x1, waiting for transfers between devices: 46.9 us -> 25.9 us  [local(): lax.all_to_all(spectra, ('sector', 'blk'), split_axis=0, concat_axis=0, t...]
    convert_element_type x2 -> x0, other arithmetic: 20.4 us -> none  [the longest x1 18 us: fourier_table(): return (value * window / math.sqrt(3.0 * NFFT / 8.0)).astype(jnp.bfloat16)]
    convert_element_type x1 -> x0, local copies, waits for them, and re-layouts: 12.1 us -> none  [segment_spectra(): return (upper + lower).astype(jnp.bfloat16)]
  transfers between devices with their start and end apart: 9 -> 1, of which waited for: 8 -> 1; matrix products, arithmetic and copies ran while one was open for 4% -> 4% of each run, Pallas kernels for 0% -> 25%
where the time goes in v1:
time: 97.2 us; the launch traced here: 96.9 us
  Pallas kernels  50.3 us (52%)
  waiting for transfers between devices  25.9 us (27%)
  starting transfers between devices  15.7 us (16%)
  local copies, waits for them, and re-layouts  3.77 us (4%)
  other arithmetic  1.17 us (1%)
    all_to_all x1, waiting for transfers between devices, local(): lax.all_to_all(spectra, ('sector', 'blk'), split_axis=0, concat_axis=0, t...  25.9 us
    pallas_call x1, Pallas kernels, steering(): pl.pallas_call(steer_body, grid=(total_mics // STEER_COLS,), out_shape=ja...  24.5 us
    all_to_all x1, starting transfers between devices, local(): lax.all_to_all(spectra, ('sector', 'blk'), split_axis=0, concat_axis=0, t...  15.7 us
    pallas_call x1, Pallas kernels, local_spectra(): pl.pallas_call(spectra_body, out_shape=jax.ShapeDtypeStruct((owners, mics...  14.1 us
    pallas_call x1, Pallas kernels, beam(): pl.pallas_call(body, grid=(total // BEAM_ROWS,), out_shape=jax.ShapeDtype...  11.7 us
  transfers between devices with their start and end apart: 1, of which 1 were waited for; matrix products, arithmetic and copies ran while one was open for 4% of the time, Pallas kernels for 25%

profile of v1, /device:TPU:1, one launch (start us, length us, event | category | flops | bytes accessed | tf_op | source)
XLA Modules:
  0.0 96.9 jit_solution(11348469322767484620)
XLA Ops:
  0.0 14.1 %spectra.1 = bf16[256,32,128]{2,1,0:T(8,128)(2,1)} custom-call(s32[2]{0:T(128)} %offsets_ref.1, bf16[2,32,8192]{2,1,0:T(8,128)(2,1)} %signal_ref.1, f32[2,8192]{1,0:T(2,128)} %fraction_ref.1, bf16[1024,512]{1,0:T(8,128)(2,1)} %constant.18.clone.upper_ref, bf16[1024,512]{1,0:T(8,128)(2,1)} %constant.19.clone.lower_ref), custom_call_target="tpu_custom_call" | custom-call | tf_op jit(solution)/shard_map/spectra/pallas_call | solution.py:118
  14.1 0.0 copy-start.1
  14.1 0.0 copy-start.2
  14.1 15.7 %all-to-all-start = ((bf16[256,32,128]{2,1,0:T(8,128)(2,1)}), bf16[256,32,128]{2,1,0:T(8,128)(2,1)S(1)}, u32[]{:S(2)}, u32[]{:S(2)}) async-start(bf16[256,32,128]{2,1,0:T(8,128)(2,1)} %spectra.1), calls=%async_computation | async-start | bytes 4194304 | tf_op jit(solution)/shard_map/all_to_all | solution.py:291
  29.8 0.0 copy-done.1
  29.8 0.0 copy-done.2
  29.8 0.8 copy.9.across_ref
  30.6 0.8 copy.10.along_ref
  31.4 0.8 copy.8.base_ref
  32.2 0.5 fusion
  32.7 0.6 pad_maximum_fusion.cycle_ref
  33.4 24.5 %steer.1.refs_1_ = bf16[1024,4096]{1,0:T(8,128)(2,1)} custom-call(s32[1]{0:T(128)} %bitcast.1.first_ref, f32[2,4096]{1,0:T(2,128)} %pad_maximum_fusion.cycle_ref, f32[256,1]{1,0:T(8,128)} %copy.8.base_ref, f32[256,1]{1,0:T(8,128)} %copy.9.across_ref, f32[256,1]{1,0:T(8,128)} %copy.10.along_ref), custom_call_target="tpu_custom_call" | custom-call | tf_op jit(solution)/shard_map/steer/pallas_call | solution.py:183
  57.9 25.9 %all-to-all-done = bf16[256,32,128]{2,1,0:T(8,128)(2,1)S(1)} async-done(((bf16[256,32,128]{2,1,0:T(8,128)(2,1)}), bf16[256,32,128]{2,1,0:T(8,128)(2,1)S(1)}, u32[]{:S(2)}, u32[]{:S(2)}) %all-to-all-start) | async-done | bytes 2097184 | tf_op jit(solution)/shard_map/all_to_all | solution.py:291
  83.8 0.0 copy-start
  83.8 1.4 %copy-done = bf16[256,32,128]{2,1,0:T(8,128)(2,1)} copy-done((bf16[256,32,128]{2,1,0:T(8,128)(2,1)}, bf16[256,32,128]{2,1,0:T(8,128)(2,1)S(1)}, u32[]{:S(2)}) %copy-start) | copy-done | bytes 2097176
  85.2 11.7 %beam.1 = f32[2,256]{1,0:T(2,128)} custom-call(bf16[128,2,32,128]{3,2,1,0:T(8,128)(2,1)} %bitcast.5, bf16[1024,4096]{1,0:T(8,128)(2,1)} %steer.1.refs_1_), custom_call_target="tpu_custom_call" | custom-call | tf_op jit(solution)/shard_map/beam/pallas_call | solution.py:266
  (1 shorter events, 0.0 us)
Async XLA Ops:
  14.1 15.7 %copy-start.1 = (f32[256]{0:T(256)S(1)}, f32[256]{0:T(256)}, u32[]{:S(2)}) copy-start(f32[256]{0:T(256)} %param.10) | copy-start | bytes 3076
  14.1 15.7 %copy-start.2 = (f32[256]{0:T(256)S(1)}, f32[256]{0:T(256)}, u32[]{:S(2)}) copy-start(f32[256]{0:T(256)} %param.11) | copy-start | bytes 3076
  14.1 69.7 %all-to-all-start = ((bf16[256,32,128]{2,1,0:T(8,128)(2,1)}), bf16[256,32,128]{2,1,0:T(8,128)(2,1)S(1)}, u32[]{:S(2)}, u32[]{:S(2)}) async-start(bf16[256,32,128]{2,1,0:T(8,128)(2,1)} %spectra.1), calls=%async_computation | async-start | bytes 4194304 | tf_op jit(solution)/shard_map/all_to_all | solution.py:291
  83.8 1.4 %copy-start = (bf16[256,32,128]{2,1,0:T(8,128)(2,1)}, bf16[256,32,128]{2,1,0:T(8,128)(2,1)S(1)}, u32[]{:S(2)}) copy-start(bf16[256,32,128]{2,1,0:T(8,128)(2,1)S(1)} %all-to-all-done) | copy-start | bytes 6291460

commit v2 on v1

v2 whole, which is shorter than its diff:
```python
import math

import jax
import jax.numpy as jnp
import numpy as np
from jax import lax
from jax.experimental import pallas as pl
from jax.experimental.pallas import tpu as pltpu
from jax.sharding import PartitionSpec as P

NFFT = 1024
HALF = NFFT // 2
LANES = 128

wavenumber = 2.0
height = 0.5

f32 = jnp.float32
bf16 = jnp.bfloat16


def fourier_table(owners):
    sample = np.arange(NFFT)[:, None]
    per_owner = HALF // owners
    in_group = LANES // (2 * per_owner)
    column = np.arange(2 * HALF)[None, :]
    owner = column // LANES * in_group + column % in_group
    part = column // in_group % 2
    frequency = owner * per_owner + column % LANES // (2 * in_group)
    angle = (sample * frequency % NFFT) * (2.0 * math.pi / NFFT)
    window = 0.5 - 0.5 * np.cos(sample * (2.0 * math.pi / NFFT))
    value = np.where(part == 0, np.cos(angle), -np.sin(angle)) * window / math.sqrt(3.0 * NFFT / 8.0)
    return value.astype(np.float32).astype(bf16)


ROWS = 16
TABLE_COLS = 256


def gather_rows(signal_ref, fraction_ref, rows_ref):
    blocks, mics, length = signal_ref.shape
    halves = length // HALF
    row = lax.broadcasted_iota(jnp.int32, (mics, 1), 0)

    def place(part, b, segment):
        first = ((part * blocks + b) * halves + segment) * ROWS
        return slice(first, first + ROWS)

    for b in range(blocks):
        for h in range(halves):
            cols = slice(h * HALF, (h + 1) * HALF)
            weight = fraction_ref[b : b + 1, cols]
            here = signal_ref[b, :, cols].astype(f32)
            following = jnp.where(row == mics - 1, 0.0, pltpu.roll(here, mics - 1, 0))
            mixed = ((1.0 - weight) * here + weight * following).astype(bf16)
            for part in range(mics // ROWS):
                piece = mixed[part * ROWS : (part + 1) * ROWS]
                if h < halves - 1:
                    rows_ref[place(part, b, h), :HALF] = piece
                if h > 0:
                    rows_ref[place(part, b, h - 1), HALF:] = piece
        share = jnp.zeros((ROWS, NFFT), f32)
        for segment in range(halves - 1):
            cols = slice(segment * HALF, segment * HALF + NFFT)
            first = fraction_ref[b : b + 1, cols] * signal_ref[b, 0:1, cols].astype(f32)
            share = jnp.where(row[:ROWS] == segment, first, share)
        rows_ref[place(0, b, halves - 1), :] = share.astype(bf16)
        for part in range(1, mics // ROWS):
            rows_ref[place(part, b, halves - 1), :] = jnp.zeros((ROWS, NFFT), bf16)


def spectra_body(offsets_ref, signal_ref, fraction_ref, table_ref, out_ref, rows_ref):
    blocks, mics, length = signal_ref.shape
    halves = length // HALF
    slot = blocks * halves
    lane = lax.broadcasted_iota(jnp.int32, (ROWS, LANES), 1)
    row = lax.broadcasted_iota(jnp.int32, (ROWS, LANES), 0)

    @pl.when(pl.program_id(0) == 0)
    def _():
        gather_rows(signal_ref, fraction_ref, rows_ref)

    for part in range(mics // ROWS):
        rows = rows_ref[part * slot * ROWS : (part + 1) * slot * ROWS, :]
        product = jnp.dot(rows, table_ref[...], preferred_element_type=f32)
        for tile in range(TABLE_COLS // LANES):
            pieces = [product[i * ROWS : (i + 1) * ROWS, tile * LANES : (tile + 1) * LANES] for i in range(slot)]
            if part == 1:
                for b in range(blocks):
                    i = b * halves + halves - 1
                    hop = (offsets_ref[b] // mics).astype(f32)
                    within = (offsets_ref[b] % mics).astype(f32)
                    pieces[i] = jnp.where(row == 0, hop, jnp.where(row == 1, within, pieces[i]))
            pieces = [piece.astype(bf16) for piece in pieces]
            step = 1
            while step < slot:
                odd = lane // step % 2 == 1
                for i in range(slot):
                    if i & step == 0:
                        a, z = pieces[i], pieces[i | step]
                        pieces[i] = jnp.where(odd, pltpu.roll(z, step, 1), a)
                        pieces[i | step] = jnp.where(odd, z, pltpu.roll(a, LANES - step, 1))
                step *= 2
            for i in range(slot):
                out_ref[tile * slot + i, part * ROWS : (part + 1) * ROWS, :] = pieces[i].astype(bf16)


def local_spectra(signal, offsets, fraction, owners):
    blocks, mics, length = signal.shape
    rows = mics * blocks * (length // HALF)
    per_step = owners * TABLE_COLS // NFFT
    return pl.pallas_call(
        spectra_body,
        grid=(NFFT // TABLE_COLS,),
        out_shape=jax.ShapeDtypeStruct((owners, mics, LANES), bf16),
        in_specs=[
            pl.BlockSpec(memory_space=pltpu.SMEM),
            pl.BlockSpec(signal.shape, lambda i: (0, 0, 0)),
            pl.BlockSpec(fraction.shape, lambda i: (0, 0)),
            pl.BlockSpec((NFFT, TABLE_COLS), lambda i: (0, i)),
        ],
        out_specs=pl.BlockSpec((per_step, mics, LANES), lambda i: (i, 0, 0)),
        scratch_shapes=[pltpu.VMEM((rows, NFFT), bf16)],
        name="spectra",
    )(offsets, signal, fraction, jnp.asarray(fourier_table(owners)))


def cos_sin(phase):
    turns = jnp.round(phase * (1.0 / math.pi))
    rest = phase - turns * 3.140625
    rest = rest - turns * 9.67502593994140625e-4
    rest = rest - turns * 1.509957990978376432e-7
    half = turns * 0.5
    sign = 1.0 - 4.0 * (half - jnp.floor(half))
    square = rest * rest
    cosine = 1.0 / math.factorial(12)
    for order in (10, 8, 6, 4, 2, 0):
        cosine = cosine * square + (-1.0) ** (order // 2) / math.factorial(order)
    sine = -1.0 / math.factorial(11)
    for order in (9, 7, 5, 3, 1):
        sine = sine * square + (-1.0) ** (order // 2) / math.factorial(order)
    return sign * cosine, sign * rest * sine


STEER_COLS = 512


def steer_body(first_ref, cycle_ref, base_ref, across_ref, along_ref, out_ref):
    points = base_ref.shape[0]
    bins = out_ref.shape[0] // (2 * points)
    first = first_ref[0]
    cycle_cos = cycle_ref[0:1, :]
    cycle_sin = cycle_ref[1:2, :]

    def rows16(i, _):
        rows = pl.ds(pl.multiple_of(i * 16, 16), 16)
        squared = base_ref[rows, :] - 2.0 * (cycle_cos * across_ref[rows, :] + cycle_sin * along_ref[rows, :])
        distance = jnp.sqrt(squared)
        for j in range(bins):
            phase = wavenumber * (first + j).astype(f32) * distance
            cosine, sine = cos_sin(phase)
            place = pl.multiple_of(2 * j * points + i * 16, 16)
            out_ref[pl.ds(place, 16), :] = cosine.astype(bf16)
            place = pl.multiple_of((2 * j + 1) * points + i * 16, 16)
            out_ref[pl.ds(place, 16), :] = sine.astype(bf16)
        return 0

    lax.fori_loop(0, points // 16, rows16, 0)


def steering(first, bins, radius, azimuth, total_mics):
    turn = lax.iota(jnp.int32, total_mics).astype(f32) * (2.0 * math.pi / total_mics)
    cycle = jnp.stack([jnp.cos(turn), jnp.sin(turn)])
    points = radius.shape[0]
    base = (1.0 + height * height + radius * radius)[:, None]
    across = (radius * jnp.cos(azimuth))[:, None]
    along = (radius * jnp.sin(azimuth))[:, None]
    column = pl.BlockSpec((points, 1), lambda i: (0, 0))
    return pl.pallas_call(
        steer_body,
        grid=(total_mics // STEER_COLS,),
        out_shape=jax.ShapeDtypeStruct((bins * 2 * points, total_mics), bf16),
        in_specs=[
            pl.BlockSpec(memory_space=pltpu.SMEM),
            pl.BlockSpec((2, STEER_COLS), lambda i: (0, i)),
            column,
            column,
            column,
        ],
        out_specs=pl.BlockSpec((bins * 2 * points, STEER_COLS), lambda i: (0, i)),
        name="steer",
    )(first.reshape(1), cycle, base, across, along)


BEAM_ROWS = 1024
PIECE = 512
LANDINGS = 4


def beam_body(moved_ref, steer_ref, out_ref, land_ref, wide_ref, start_ref, sum_ref, copied, *, mics, blocks, halves, groups, scale):
    step = pl.program_id(0)
    sources = moved_ref.shape[0] // groups
    total = sources * mics
    lane = lax.broadcasted_iota(jnp.int32, (1, LANES), 1)
    row8 = lax.broadcasted_iota(jnp.int32, (8, LANES), 0)
    spare = lane % halves == halves - 1
    of_block = lane // halves % blocks

    @pl.when(step == 0)
    def _():
        share = moved_ref.shape[0] // LANDINGS
        copies = []
        for i in range(LANDINGS):
            place = pl.ds(i * share, share)
            copies.append(pltpu.make_async_copy(moved_ref.at[place], land_ref.at[place], copied.at[i]))
            copies[-1].start()

        def carried(x):
            low = pltpu.roll(jnp.where(spare, x[0:8], 0.0), LANES - halves + 1, 1, stride=1, stride_axis=0)
            high = pltpu.roll(jnp.where(spare, x[8:16], 0.0), LANES - halves + 9, 1, stride=1, stride_axis=0)
            return jnp.sum(low + high, 0, keepdims=True)

        copies[0].wait()
        heads = [land_ref[group].astype(f32) for group in range(groups)]
        which = lax.broadcasted_iota(jnp.int32, (mics, LANES), 0)
        for group in range(groups):
            for b in range(blocks):
                mine = spare & (of_block == b) & (lane // (blocks * halves) == 0)
                number = jnp.where(which == halves, heads[group] * mics, jnp.where(which == halves + 1, heads[group], 0.0))
                start_ref[group * blocks + b] = jnp.sum(jnp.where(mine, number, 0.0)).astype(jnp.int32)
        for copy in copies[1:]:
            copy.wait()

        def one_source(i, after):
            source = sources - 1 - i
            before = []
            for group in range(groups):
                x = land_ref[source * groups + group].astype(f32)
                first = pl.multiple_of(source * mics, mics)
                wide_ref[group, pl.ds(first, mics - 8), :] = x[: mics - 8]
                wide_ref[group, pl.ds(first + mics - 8, 8), :] = x[mics - 8 :] + jnp.where(row8 == 7, after[group], 0.0)
                before.append(carried(x))
            return tuple(before)

        lax.fori_loop(0, sources, one_source, tuple(carried(x) for x in heads), unroll=8)
        for group in range(groups):
            wide_ref[group, total : total + PIECE, :] = wide_ref[group, 0:PIECE, :]
        sum_ref[...] = jnp.zeros(sum_ref.shape, f32)

    stacked = []
    for piece in range(BEAM_ROWS // PIECE):
        columns = []
        for group in range(groups):
            start = [(start_ref[group * blocks + b] + step * BEAM_ROWS + piece * PIECE) % total for b in range(blocks)]
            rows = [wide_ref[group, pl.ds(s, PIECE), :] for s in start]
            columns.append(jnp.where(of_block == 0, rows[0], rows[1]).astype(bf16))
        stacked.append(jnp.concatenate(columns, 1))
    sum_ref[...] += jnp.dot(steer_ref[...], jnp.concatenate(stacked, 0), preferred_element_type=f32)

    @pl.when(step == pl.num_programs(0) - 1)
    def _():
        points = out_ref.shape[1]
        slot = blocks * halves
        imaginary = lane // slot % 2 == 1
        for j in range(out_ref.shape[0]):
            power = jnp.zeros((points, LANES), f32)
            for group in range(groups):
                cols = slice(group * LANES, (group + 1) * LANES)
                by_cos = sum_ref[2 * j * points : (2 * j + 1) * points, cols]
                by_sin = sum_ref[(2 * j + 1) * points : (2 * j + 2) * points, cols]
                other = jnp.where(imaginary, -pltpu.roll(by_sin, slot, 1), pltpu.roll(by_sin, LANES - slot, 1))
                both = by_cos + other
                power = power + both * both
            power = jnp.where(~spare & (lane // (2 * slot) == j), power, 0.0)
            out_ref[j : j + 1, :] = jnp.sum(power.T, 0, keepdims=True) * scale


def beam(moved, steer, mics, blocks, halves, groups, points, scale):
    total = moved.shape[0] // groups * mics
    bins = steer.shape[0] // (2 * points)
    body = lambda *refs: beam_body(*refs, mics=mics, blocks=blocks, halves=halves, groups=groups, scale=scale)
    return pl.pallas_call(
        body,
        grid=(total // BEAM_ROWS,),
        out_shape=jax.ShapeDtypeStruct((bins, points), f32),
        in_specs=[
            pl.BlockSpec(memory_space=pl.ANY),
            pl.BlockSpec((steer.shape[0], BEAM_ROWS), lambda i: (0, i)),
        ],
        out_specs=pl.BlockSpec((bins, points), lambda i: (0, 0)),
        scratch_shapes=[
            pltpu.VMEM(moved.shape, bf16),
            pltpu.VMEM((groups, total + PIECE, LANES), f32),
            pltpu.SMEM((groups * blocks,), jnp.int32),
            pltpu.VMEM((steer.shape[0], groups * LANES), f32),
            pltpu.SemaphoreType.DMA((LANDINGS,)),
        ],
        name="beam",
    )(moved, steer)


def local(signal, offsets, fraction, radius, azimuth):
    blocks, mics, length = signal.shape
    sectors, groups = lax.axis_size("sector"), lax.axis_size("blk")
    owners = sectors * groups
    halves = length // HALF
    bins = HALF // owners
    spectra = local_spectra(signal, offsets, fraction, owners)
    moved = lax.all_to_all(spectra, ("sector", "blk"), split_axis=0, concat_axis=0, tiled=True)
    first = (lax.axis_index("sector") * groups + lax.axis_index("blk")) * bins
    total_mics = sectors * mics
    steer = steering(first, bins, radius, azimuth, total_mics)
    scale = 1.0 / (total_mics * blocks * (halves - 1) * groups)
    return beam(moved, steer, mics, blocks, halves, groups, radius.shape[0], scale)


def solution(mesh):
    return jax.shard_map(
        local,
        mesh=mesh,
        in_specs=(P("blk", "sector", None), P("blk"), P("blk", None), P(), P()),
        out_specs=P(("sector", "blk"), None),
        check_vma=False,
    )
```

time: 97.2 us -> 89.9 us (0.925)
  Pallas kernels: 50.3 us -> 43.1 us
    pallas_call x1, Pallas kernels: 14.1 us -> 8.34 us  [local_spectra(): pl.pallas_call(spectra_body, grid=(NFFT // TABLE_COLS,), out_shape=jax.Sh...]
    pallas_call x1, Pallas kernels: 11.7 us -> 10.2 us  [beam(): pl.pallas_call(body, grid=(total // BEAM_ROWS,), out_shape=jax.ShapeDtype...]
  transfers between devices with their start and end apart: 1 -> 1, of which waited for: 1 -> 1; matrix products, arithmetic and copies ran while one was open for 4% -> 4% of each run, Pallas kernels for 25% -> 27%
where the time goes in v2:
time: 89.9 us; the launch traced here: 89.6 us
  Pallas kernels  43.1 us (48%)
  waiting for transfers between devices  25.9 us (29%)
  starting transfers between devices  15.6 us (17%)
  local copies, waits for them, and re-layouts  3.77 us (4%)
  other arithmetic  1.17 us (1%)
    all_to_all x1, waiting for transfers between devices, local(): lax.all_to_all(spectra, ('sector', 'blk'), split_axis=0, concat_axis=0, t...  25.9 us
    pallas_call x1, Pallas kernels, steering(): pl.pallas_call(steer_body, grid=(total_mics // STEER_COLS,), out_shape=ja...  24.5 us
    all_to_all x1, starting transfers between devices, local(): lax.all_to_all(spectra, ('sector', 'blk'), split_axis=0, concat_axis=0, t...  15.6 us
    pallas_call x1, Pallas kernels, beam(): pl.pallas_call(body, grid=(total // BEAM_ROWS,), out_shape=jax.ShapeDtype...  10.2 us
    pallas_call x1, Pallas kernels, local_spectra(): pl.pallas_call(spectra_body, grid=(NFFT // TABLE_COLS,), out_shape=jax.Sh...  8.34 us
  transfers between devices with their start and end apart: 1, of which 1 were waited for; matrix products, arithmetic and copies ran while one was open for 4% of the time, Pallas kernels for 27%

profile of v2, /device:TPU:1, one launch (start us, length us, event | category | flops | bytes accessed | tf_op | source)
XLA Modules:
  0.0 89.6 jit_solution(11134508396778787813)
XLA Ops:
  0.0 8.3 %spectra.1 = bf16[256,32,128]{2,1,0:T(8,128)(2,1)} custom-call(s32[2]{0:T(128)} %offsets_ref.1, bf16[2,32,8192]{2,1,0:T(8,128)(2,1)} %signal_ref.1, f32[2,8192]{1,0:T(2,128)} %fraction_ref.1, bf16[1024,1024]{1,0:T(8,128)(2,1)} %constant.16.clone.table_ref), custom_call_target="tpu_custom_call" | custom-call | tf_op jit(solution)/shard_map/spectra/pallas_call | solution.py:112
  8.3 0.0 copy-start.1
  8.3 0.0 copy-start.2
  8.3 15.6 %all-to-all-start = ((bf16[256,32,128]{2,1,0:T(8,128)(2,1)}), bf16[256,32,128]{2,1,0:T(8,128)(2,1)S(1)}, u32[]{:S(2)}, u32[]{:S(2)}) async-start(bf16[256,32,128]{2,1,0:T(8,128)(2,1)} %spectra.1), calls=%async_computation | async-start | bytes 4194304 | tf_op jit(solution)/shard_map/all_to_all | solution.py:309
  24.0 0.0 copy-done.1
  24.0 0.0 copy-done.2
  24.1 0.8 copy.8.across_ref
  24.9 0.8 copy.9.along_ref
  25.7 0.8 copy.7.base_ref
  26.5 0.5 fusion
  27.0 0.6 pad_maximum_fusion.cycle_ref
  27.6 24.5 %steer.1.refs_1_ = bf16[1024,4096]{1,0:T(8,128)(2,1)} custom-call(s32[1]{0:T(128)} %bitcast.first_ref, f32[2,4096]{1,0:T(2,128)} %pad_maximum_fusion.cycle_ref, f32[256,1]{1,0:T(8,128)} %copy.7.base_ref, f32[256,1]{1,0:T(8,128)} %copy.8.across_ref, f32[256,1]{1,0:T(8,128)} %copy.9.along_ref), custom_call_target="tpu_custom_call" | custom-call | tf_op jit(solution)/shard_map/steer/pallas_call | solution.py:179
  52.1 25.9 %all-to-all-done.refs_0_ = bf16[256,32,128]{2,1,0:T(8,128)(2,1)S(1)} async-done(((bf16[256,32,128]{2,1,0:T(8,128)(2,1)}), bf16[256,32,128]{2,1,0:T(8,128)(2,1)S(1)}, u32[]{:S(2)}, u32[]{:S(2)}) %all-to-all-start) | async-done | bytes 2097184 | tf_op jit(solution)/shard_map/all_to_all | solution.py:309
  78.1 0.0 copy-start
  78.1 1.4 %copy-done = bf16[256,32,128]{2,1,0:T(8,128)(2,1)} copy-done((bf16[256,32,128]{2,1,0:T(8,128)(2,1)}, bf16[256,32,128]{2,1,0:T(8,128)(2,1)S(1)}, u32[]{:S(2)}) %copy-start) | copy-done | bytes 2097176
  79.4 10.2 %beam.1 = f32[2,256]{1,0:T(2,128)} custom-call(bf16[256,32,128]{2,1,0:T(8,128)(2,1)} %copy-done, bf16[1024,4096]{1,0:T(8,128)(2,1)} %steer.1.refs_1_), custom_call_target="tpu_custom_call" | custom-call | tf_op jit(solution)/shard_map/beam/pallas_call | solution.py:282
  (1 shorter events, 0.0 us)
Async XLA Ops:
  8.3 15.7 %copy-start.1 = (f32[256]{0:T(256)S(1)}, f32[256]{0:T(256)}, u32[]{:S(2)}) copy-start(f32[256]{0:T(256)} %param.9) | copy-start | bytes 3076
  8.3 15.7 %copy-start.2 = (f32[256]{0:T(256)S(1)}, f32[256]{0:T(256)}, u32[]{:S(2)}) copy-start(f32[256]{0:T(256)} %param.10) | copy-start | bytes 3076
  8.3 69.7 %all-to-all-start = ((bf16[256,32,128]{2,1,0:T(8,128)(2,1)}), bf16[256,32,128]{2,1,0:T(8,128)(2,1)S(1)}, u32[]{:S(2)}, u32[]{:S(2)}) async-start(bf16[256,32,128]{2,1,0:T(8,128)(2,1)} %spectra.1), calls=%async_computation | async-start | bytes 4194304 | tf_op jit(solution)/shard_map/all_to_all | solution.py:309
  78.1 1.4 %copy-start = (bf16[256,32,128]{2,1,0:T(8,128)(2,1)}, bf16[256,32,128]{2,1,0:T(8,128)(2,1)S(1)}, u32[]{:S(2)}) copy-start(bf16[256,32,128]{2,1,0:T(8,128)(2,1)S(1)} %all-to-all-done.refs_0_) | copy-start | bytes 6291460

commit v3 on v2

--- a/solution.py
+++ b/solution.py
@@ -51,7 +51,9 @@
             cols = slice(h * HALF, (h + 1) * HALF)
             weight = fraction_ref[b : b + 1, cols]
             here = signal_ref[b, :, cols].astype(f32)
-            following = jnp.where(row == mics - 1, 0.0, pltpu.roll(here, mics - 1, 0))
+            turned = pltpu.roll(here, mics - 1, 0)
+            ending = jnp.where(row[:8] == 7, 0.0, turned[mics - 8 :])
+            following = jnp.concatenate([turned[: mics - 8], ending], 0)
             mixed = ((1.0 - weight) * here + weight * following).astype(bf16)
             for part in range(mics // ROWS):
                 piece = mixed[part * ROWS : (part + 1) * ROWS]
@@ -92,15 +94,14 @@
                     within = (offsets_ref[b] % mics).astype(f32)
                     pieces[i] = jnp.where(row == 0, hop, jnp.where(row == 1, within, pieces[i]))
             pieces = [piece.astype(bf16) for piece in pieces]
+            pieces = [pltpu.roll(pieces[i], i, 1) if i else pieces[i] for i in range(slot)]
+            pieces = [pieces[-i % slot] for i in range(slot)]
             step = 1
             while step < slot:
                 odd = lane // step % 2 == 1
-                for i in range(slot):
-                    if i & step == 0:
-                        a, z = pieces[i], pieces[i | step]
-                        pieces[i] = jnp.where(odd, pltpu.roll(z, step, 1), a)
-                        pieces[i | step] = jnp.where(odd, z, pltpu.roll(a, LANES - step, 1))
+                pieces = [jnp.where(odd, pieces[(i - step) % slot], pieces[i]) for i in range(slot)]
                 step *= 2
+            pieces = [pltpu.roll(pieces[i], LANES - i, 1) if i else pieces[i] for i in range(slot)]
             for i in range(slot):
                 out_ref[tile * slot + i, part * ROWS : (part + 1) * ROWS, :] = pieces[i].astype(bf16)
 
@@ -194,10 +195,9 @@
 
 BEAM_ROWS = 1024
 PIECE = 512
-LANDINGS = 4
-
-
-def beam_body(moved_ref, steer_ref, out_ref, land_ref, wide_ref, start_ref, sum_ref, copied, *, mics, blocks, halves, groups, scale):
+
+
+def beam_body(moved_ref, steer_ref, out_ref, wide_ref, start_ref, sum_ref, *, mics, blocks, halves, groups, scale):
     step = pl.program_id(0)
     sources = moved_ref.shape[0] // groups
     total = sources * mics
@@ -208,41 +208,31 @@
 
     @pl.when(step == 0)
     def _():
-        share = moved_ref.shape[0] // LANDINGS
-        copies = []
-        for i in range(LANDINGS):
-            place = pl.ds(i * share, share)
-            copies.append(pltpu.make_async_copy(moved_ref.at[place], land_ref.at[place], copied.at[i]))
-            copies[-1].start()
-
         def carried(x):
             low = pltpu.roll(jnp.where(spare, x[0:8], 0.0), LANES - halves + 1, 1, stride=1, stride_axis=0)
             high = pltpu.roll(jnp.where(spare, x[8:16], 0.0), LANES - halves + 9, 1, stride=1, stride_axis=0)
             return jnp.sum(low + high, 0, keepdims=True)
 
-        copies[0].wait()
-        heads = [land_ref[group].astype(f32) for group in range(groups)]
+        heads = [moved_ref[group].astype(f32) for group in range(groups)]
         which = lax.broadcasted_iota(jnp.int32, (mics, LANES), 0)
         for group in range(groups):
             for b in range(blocks):
                 mine = spare & (of_block == b) & (lane // (blocks * halves) == 0)
                 number = jnp.where(which == halves, heads[group] * mics, jnp.where(which == halves + 1, heads[group], 0.0))
                 start_ref[group * blocks + b] = jnp.sum(jnp.where(mine, number, 0.0)).astype(jnp.int32)
-        for copy in copies[1:]:
-            copy.wait()
 
         def one_source(i, after):
             source = sources - 1 - i
             before = []
             for group in range(groups):
-                x = land_ref[source * groups + group].astype(f32)
+                x = moved_ref[source * groups + group].astype(f32)
                 first = pl.multiple_of(source * mics, mics)
                 wide_ref[group, pl.ds(first, mics - 8), :] = x[: mics - 8]
                 wide_ref[group, pl.ds(first + mics - 8, 8), :] = x[mics - 8 :] + jnp.where(row8 == 7, after[group], 0.0)
                 before.append(carried(x))
             return tuple(before)
 
-        lax.fori_loop(0, sources, one_source, tuple(carried(x) for x in heads), unroll=8)
+        lax.fori_loop(0, sources, one_source, tuple(carried(x) for x in heads), unroll=32)
         for group in range(groups):
             wide_ref[group, total : total + PIECE, :] = wide_ref[group, 0:PIECE, :]
         sum_ref[...] = jnp.zeros(sum_ref.shape, f32)
@@ -284,16 +274,14 @@
         grid=(total // BEAM_ROWS,),
         out_shape=jax.ShapeDtypeStruct((bins, points), f32),
         in_specs=[
-            pl.BlockSpec(memory_space=pl.ANY),
+            pl.BlockSpec(memory_space=pltpu.VMEM),
             pl.BlockSpec((steer.shape[0], BEAM_ROWS), lambda i: (0, i)),
         ],
         out_specs=pl.BlockSpec((bins, points), lambda i: (0, 0)),
         scratch_shapes=[
-            pltpu.VMEM(moved.shape, bf16),
             pltpu.VMEM((groups, total + PIECE, LANES), f32),
             pltpu.SMEM((groups * blocks,), jnp.int32),
             pltpu.VMEM((steer.shape[0], groups * LANES), f32),
-            pltpu.SemaphoreType.DMA((LANDINGS,)),
         ],
         name="beam",
     )(moved, steer)
@@ -307,6 +295,7 @@
     bins = HALF // owners
     spectra = local_spectra(signal, offsets, fraction, owners)
     moved = lax.all_to_all(spectra, ("sector", "blk"), split_axis=0, concat_axis=0, tiled=True)
+    moved = pltpu.with_memory_space_constraint(moved, pltpu.VMEM)
     first = (lax.axis_index("sector") * groups + lax.axis_index("blk")) * bins
     total_mics = sectors * mics
     steer = steering(first, bins, radius, azimuth, total_mics)

time: 89.9 us -> 84.9 us (0.944)
  Pallas kernels: 43.1 us -> 39.4 us
  local copies, waits for them, and re-layouts: 3.77 us -> 2.4 us
    pallas_call x1, Pallas kernels: 10.2 us -> 7.77 us  [beam(): pl.pallas_call(body, grid=(total // BEAM_ROWS,), out_shape=jax.ShapeDtype...]
    unnamed x6 -> x4, local copies, waits for them, and re-layouts: 1.37 us -> 0.01 us
    pallas_call x1, Pallas kernels: 8.34 us -> 7.08 us  [local_spectra(): pl.pallas_call(spectra_body, grid=(NFFT // TABLE_COLS,), out_shape=jax.Sh...]
  transfers between devices with their start and end apart: 1 -> 1, of which waited for: 1 -> 1; matrix products, arithmetic and copies ran while one was open for 4% -> 4% of each run, Pallas kernels for 27% -> 29%
where the time goes in v3:
time: 84.9 us; the launch traced here: 84.6 us
  Pallas kernels  39.4 us (46%)
  waiting for transfers between devices  25.9 us (31%)
  starting transfers between devices  15.6 us (18%)
  local copies, waits for them, and re-layouts  2.4 us (3%)
  other arithmetic  1.15 us (1%)
    all_to_all x1, waiting for transfers between devices, local(): lax.all_to_all(spectra, ('sector', 'blk'), split_axis=0, concat_axis=0, t...  25.9 us
    pallas_call x1, Pallas kernels, steering(): pl.pallas_call(steer_body, grid=(total_mics // STEER_COLS,), out_shape=ja...  24.6 us
    all_to_all x1, starting transfers between devices, local(): lax.all_to_all(spectra, ('sector', 'blk'), split_axis=0, concat_axis=0, t...  15.6 us
    pallas_call x1, Pallas kernels, beam(): pl.pallas_call(body, grid=(total // BEAM_ROWS,), out_shape=jax.ShapeDtype...  7.77 us
    pallas_call x1, Pallas kernels, local_spectra(): pl.pallas_call(spectra_body, grid=(NFFT // TABLE_COLS,), out_shape=jax.Sh...  7.08 us
  transfers between devices with their start and end apart: 1, of which 1 were waited for; matrix products, arithmetic and copies ran while one was open for 4% of the time, Pallas kernels for 29%

profile of v3, /device:TPU:1, one launch (start us, length us, event | category | flops | bytes accessed | tf_op | source)
XLA Modules:
  0.0 84.6 jit_solution(16146467329486575688)
XLA Ops:
  0.0 7.1 %spectra.1 = bf16[256,32,128]{2,1,0:T(8,128)(2,1)} custom-call(s32[2]{0:T(128)} %offsets_ref.1, bf16[2,32,8192]{2,1,0:T(8,128)(2,1)} %signal_ref.1, f32[2,8192]{1,0:T(2,128)} %fraction_ref.1, bf16[1024,1024]{1,0:T(8,128)(2,1)} %constant.16.clone.table_ref), custom_call_target="tpu_custom_call" | custom-call | tf_op jit(solution)/shard_map/spectra/pallas_call | solution.py:113
  7.1 0.0 copy-start
  7.1 0.0 copy-start.1
  7.1 15.6 %all-to-all-start = ((bf16[256,32,128]{2,1,0:T(8,128)(2,1)}), bf16[256,32,128]{2,1,0:T(8,128)(2,1)S(1)}, u32[]{:S(2)}, u32[]{:S(2)}) async-start(bf16[256,32,128]{2,1,0:T(8,128)(2,1)} %spectra.1), calls=%async_computation | async-start | bytes 4194304 | tf_op jit(solution)/shard_map/all_to_all | solution.py:297
  22.7 0.0 copy-done
  22.8 0.0 copy-done.1
  22.8 0.8 copy.8.across_ref
  23.6 0.8 copy.9.along_ref
  24.4 0.8 copy.7.base_ref
  25.2 0.5 fusion
  25.7 0.6 pad_maximum_fusion.cycle_ref
  26.3 24.6 %steer.1.refs_1_ = bf16[1024,4096]{1,0:T(8,128)(2,1)} custom-call(s32[1]{0:T(128)} %bitcast.first_ref, f32[2,4096]{1,0:T(2,128)} %pad_maximum_fusion.cycle_ref, f32[256,1]{1,0:T(8,128)} %copy.7.base_ref, f32[256,1]{1,0:T(8,128)} %copy.8.across_ref, f32[256,1]{1,0:T(8,128)} %copy.9.along_ref), custom_call_target="tpu_custom_call" | custom-call | tf_op jit(solution)/shard_map/steer/pallas_call | solution.py:180
  50.9 25.9 %all-to-all-done.refs_0_ = bf16[256,32,128]{2,1,0:T(8,128)(2,1)S(1)} async-done(((bf16[256,32,128]{2,1,0:T(8,128)(2,1)}), bf16[256,32,128]{2,1,0:T(8,128)(2,1)S(1)}, u32[]{:S(2)}, u32[]{:S(2)}) %all-to-all-start) | async-done | bytes 2097184 | tf_op jit(solution)/shard_map/all_to_all | solution.py:297
  76.8 7.8 %beam.1 = f32[2,256]{1,0:T(2,128)} custom-call(bf16[256,32,128]{2,1,0:T(8,128)(2,1)S(1)} %all-to-all-done.refs_0_, bf16[1024,4096]{1,0:T(8,128)(2,1)} %steer.1.refs_1_), custom_call_target="tpu_custom_call" | custom-call | tf_op jit(solution)/shard_map/beam/pallas_call | solution.py:272
  (1 shorter events, 0.0 us)
Async XLA Ops:
  7.1 15.7 %copy-start = (f32[256]{0:T(256)S(1)}, f32[256]{0:T(256)}, u32[]{:S(2)}) copy-start(f32[256]{0:T(256)} %param.9) | copy-start | bytes 3076
  7.1 15.7 %copy-start.1 = (f32[256]{0:T(256)S(1)}, f32[256]{0:T(256)}, u32[]{:S(2)}) copy-start(f32[256]{0:T(256)} %param.10) | copy-start | bytes 3076
  7.1 69.7 %all-to-all-start = ((bf16[256,32,128]{2,1,0:T(8,128)(2,1)}), bf16[256,32,128]{2,1,0:T(8,128)(2,1)S(1)}, u32[]{:S(2)}, u32[]{:S(2)}) async-start(bf16[256,32,128]{2,1,0:T(8,128)(2,1)} %spectra.1), calls=%async_computation | async-start | bytes 4194304 | tf_op jit(solution)/shard_map/all_to_all | solution.py:297

commit v4 on v3

v4 whole, which is shorter than its diff:
```python
import math

import jax
import jax.numpy as jnp
import numpy as np
from jax import lax
from jax.experimental import pallas as pl
from jax.experimental.pallas import tpu as pltpu
from jax.sharding import PartitionSpec as P

NFFT = 1024
HALF = NFFT // 2
LANES = 128

wavenumber = 2.0
height = 0.5

f32 = jnp.float32
bf16 = jnp.bfloat16


def fourier_table(owners):
    sample = np.arange(NFFT)[:, None]
    per_owner = HALF // owners
    in_group = LANES // (2 * per_owner)
    column = np.arange(2 * HALF)[None, :]
    owner = column // LANES * in_group + column % in_group
    part = column // in_group % 2
    frequency = owner * per_owner + column % LANES // (2 * in_group)
    angle = (sample * frequency % NFFT) * (2.0 * math.pi / NFFT)
    window = 0.5 - 0.5 * np.cos(sample * (2.0 * math.pi / NFFT))
    value = np.where(part == 0, np.cos(angle), -np.sin(angle)) * window / math.sqrt(3.0 * NFFT / 8.0)
    return value.astype(np.float32).astype(bf16)


ROWS = 16
TABLE_COLS = 256


def gather_rows(b, signal_ref, fraction_ref, rows_ref):
    blocks, mics, length = signal_ref.shape
    halves = length // HALF
    row = lax.broadcasted_iota(jnp.int32, (mics, 1), 0)

    def place(part, b, segment):
        first = ((part * blocks + b) * halves + segment) * ROWS
        return slice(first, first + ROWS)

    for h in range(halves):
        cols = slice(h * HALF, (h + 1) * HALF)
        weight = fraction_ref[b : b + 1, cols]
        here = signal_ref[b, :, cols].astype(f32)
        turned = pltpu.roll(here, mics - 1, 0)
        ending = jnp.where(row[:8] == 7, 0.0, turned[mics - 8 :])
        following = jnp.concatenate([turned[: mics - 8], ending], 0)
        mixed = ((1.0 - weight) * here + weight * following).astype(bf16)
        for part in range(mics // ROWS):
            piece = mixed[part * ROWS : (part + 1) * ROWS]
            if h < halves - 1:
                rows_ref[place(part, b, h), :HALF] = piece
            if h > 0:
                rows_ref[place(part, b, h - 1), HALF:] = piece
    share = jnp.zeros((ROWS, NFFT), f32)
    for segment in range(halves - 1):
        cols = slice(segment * HALF, segment * HALF + NFFT)
        first = fraction_ref[b : b + 1, cols] * signal_ref[b, 0:1, cols].astype(f32)
        share = jnp.where(row[:ROWS] == segment, first, share)
    rows_ref[place(0, b, halves - 1), :] = share.astype(bf16)
    for part in range(1, mics // ROWS):
        rows_ref[place(part, b, halves - 1), :] = jnp.zeros((ROWS, NFFT), bf16)


def spectra_body(offsets_ref, signal_hbm, fraction_hbm, table_hbm, out_hbm, signal_ref, fraction_ref, table_ref, rows_ref, out_ref, copied):
    blocks, mics, length = signal_ref.shape
    halves = length // HALF
    slot = blocks * halves
    lane = lax.broadcasted_iota(jnp.int32, (ROWS, LANES), 1)
    row = lax.broadcasted_iota(jnp.int32, (ROWS, LANES), 0)

    pairs = [(fraction_hbm, fraction_ref)]
    pairs += [(signal_hbm.at[b], signal_ref.at[b]) for b in range(blocks)]
    pairs += [(table_hbm.at[i], table_ref.at[i]) for i in range(table_ref.shape[0])]
    copies = [pltpu.make_async_copy(source, target, copied.at[i]) for i, (source, target) in enumerate(pairs)]
    for copy in copies:
        copy.start()
    copies[0].wait()
    for b in range(blocks):
        copies[1 + b].wait()
        gather_rows(b, signal_ref, fraction_ref, rows_ref)
    columns = table_ref.shape[0]
    share = out_ref.shape[0] // columns
    leaving = []
    for i in range(columns):
        copies[1 + blocks + i].wait()
        spectra_columns(i, offsets_ref, table_ref, rows_ref, out_ref, lane, row, blocks, mics, halves, slot)
        place = pl.ds(i * share, share)
        leaving.append(pltpu.make_async_copy(out_ref.at[place], out_hbm.at[place], copied.at[len(copies) + i]))
        leaving[-1].start()
    for copy in leaving:
        copy.wait()


def spectra_columns(column, offsets_ref, table_ref, rows_ref, out_ref, lane, row, blocks, mics, halves, slot):
    first = column * (TABLE_COLS // LANES) * slot
    for part in range(mics // ROWS):
        rows = rows_ref[part * slot * ROWS : (part + 1) * slot * ROWS, :]
        product = jnp.dot(rows, table_ref[column], preferred_element_type=f32)
        for tile in range(TABLE_COLS // LANES):
            pieces = [product[i * ROWS : (i + 1) * ROWS, tile * LANES : (tile + 1) * LANES] for i in range(slot)]
            if part == 1:
                for b in range(blocks):
                    i = b * halves + halves - 1
                    hop = (offsets_ref[b] // mics).astype(f32)
                    within = (offsets_ref[b] % mics).astype(f32)
                    pieces[i] = jnp.where(row == 0, hop, jnp.where(row == 1, within, pieces[i]))
            pieces = [piece.astype(bf16) for piece in pieces]
            pieces = [pltpu.roll(pieces[i], i, 1) if i else pieces[i] for i in range(slot)]
            pieces = [pieces[-i % slot] for i in range(slot)]
            step = 1
            while step < slot:
                odd = lane // step % 2 == 1
                pieces = [jnp.where(odd, pieces[(i - step) % slot], pieces[i]) for i in range(slot)]
                step *= 2
            pieces = [pltpu.roll(pieces[i], LANES - i, 1) if i else pieces[i] for i in range(slot)]
            for i in range(slot):
                out_ref[first + tile * slot + i, part * ROWS : (part + 1) * ROWS, :] = pieces[i].astype(bf16)


def local_spectra(signal, offsets, fraction, owners):
    blocks, mics, length = signal.shape
    rows = mics * blocks * (length // HALF)
    table = fourier_table(owners).reshape(NFFT, NFFT // TABLE_COLS, TABLE_COLS).transpose(1, 0, 2)
    hbm = pl.BlockSpec(memory_space=pltpu.HBM)
    return pl.pallas_call(
        spectra_body,
        out_shape=jax.ShapeDtypeStruct((owners, mics, LANES), bf16),
        in_specs=[pl.BlockSpec(memory_space=pltpu.SMEM), hbm, hbm, hbm],
        out_specs=hbm,
        scratch_shapes=[
            pltpu.VMEM(signal.shape, bf16),
            pltpu.VMEM(fraction.shape, f32),
            pltpu.VMEM(table.shape, bf16),
            pltpu.VMEM((rows, NFFT), bf16),
            pltpu.VMEM((owners, mics, LANES), bf16),
            pltpu.SemaphoreType.DMA((1 + blocks + 2 * table.shape[0],)),
        ],
        name="spectra",
    )(offsets, signal, fraction, jnp.asarray(table))


def cos_sin(phase):
    turns = jnp.round(phase * (1.0 / math.pi))
    rest = phase - turns * 3.140625
    rest = rest - turns * 9.67502593994140625e-4
    rest = rest - turns * 1.509957990978376432e-7
    half = turns * 0.5
    sign = 1.0 - 4.0 * (half - jnp.floor(half))
    square = rest * rest
    cosine = 1.0 / math.factorial(12)
    for order in (10, 8, 6, 4, 2, 0):
        cosine = cosine * square + (-1.0) ** (order // 2) / math.factorial(order)
    sine = -1.0 / math.factorial(11)
    for order in (9, 7, 5, 3, 1):
        sine = sine * square + (-1.0) ** (order // 2) / math.factorial(order)
    return sign * cosine, sign * rest * sine


STEER_COLS = 1024


def steer_body(first_ref, cycle_ref, base_ref, across_ref, along_ref, out_ref):
    points = base_ref.shape[0]
    bins = out_ref.shape[1] // (2 * points)
    first = first_ref[0]
    cycle_cos = cycle_ref[0:1, :]
    cycle_sin = cycle_ref[1:2, :]

    def rows16(i, _):
        rows = pl.ds(pl.multiple_of(i * 16, 16), 16)
        squared = base_ref[rows, :] - 2.0 * (cycle_cos * across_ref[rows, :] + cycle_sin * along_ref[rows, :])
        distance = jnp.sqrt(squared)
        for j in range(bins):
            phase = wavenumber * (first + j).astype(f32) * distance
            cosine, sine = cos_sin(phase)
            place = pl.multiple_of(2 * j * points + i * 16, 16)
            out_ref[0, pl.ds(place, 16), :] = cosine.astype(bf16)
            place = pl.multiple_of((2 * j + 1) * points + i * 16, 16)
            out_ref[0, pl.ds(place, 16), :] = sine.astype(bf16)
        return 0

    lax.fori_loop(0, points // 16, rows16, 0)


def steering(first, bins, radius, azimuth, total_mics):
    turn = lax.iota(jnp.int32, total_mics).astype(f32) * (2.0 * math.pi / total_mics)
    cycle = jnp.stack([jnp.cos(turn), jnp.sin(turn)])
    points = radius.shape[0]
    base = (1.0 + height * height + radius * radius)[:, None]
    across = (radius * jnp.cos(azimuth))[:, None]
    along = (radius * jnp.sin(azimuth))[:, None]
    column = pl.BlockSpec((points, 1), lambda i: (0, 0))
    return pl.pallas_call(
        steer_body,
        grid=(total_mics // STEER_COLS,),
        out_shape=jax.ShapeDtypeStruct((total_mics // STEER_COLS, bins * 2 * points, STEER_COLS), bf16),
        in_specs=[
            pl.BlockSpec(memory_space=pltpu.SMEM),
            pl.BlockSpec((2, STEER_COLS), lambda i: (0, i)),
            column,
            column,
            column,
        ],
        out_specs=pl.BlockSpec((1, bins * 2 * points, STEER_COLS), lambda i: (i, 0, 0)),
        name="steer",
    )(first.reshape(1), cycle, base, across, along)


PIECE = 512


def beam_body(moved_ref, steer_hbm, out_ref, wide_ref, rows_ref, sum_ref, steer_ref, copied, *, mics, blocks, halves, groups, scale):
    chunks = steer_ref.shape[0]
    copies = [pltpu.make_async_copy(steer_hbm.at[i], steer_ref.at[i], copied.at[i]) for i in range(chunks)]
    for copy in copies:
        copy.start()
    sources = moved_ref.shape[0] // groups
    total = sources * mics
    lane = lax.broadcasted_iota(jnp.int32, (1, LANES), 1)
    row8 = lax.broadcasted_iota(jnp.int32, (8, LANES), 0)
    spare = lane % halves == halves - 1
    of_block = lane // halves % blocks

    def carried(x):
        low = pltpu.roll(jnp.where(spare, x[0:8], 0.0), LANES - halves + 1, 1, stride=1, stride_axis=0)
        high = pltpu.roll(jnp.where(spare, x[8:16], 0.0), LANES - halves + 9, 1, stride=1, stride_axis=0)
        return jnp.sum(low + high, 0, keepdims=True)

    heads = [moved_ref[group].astype(f32) for group in range(groups)]
    starts = {}
    which = lax.broadcasted_iota(jnp.int32, (mics, LANES), 0)
    for group in range(groups):
        for b in range(blocks):
            mine = spare & (of_block == b) & (lane // (blocks * halves) == 0)
            number = jnp.where(which == halves, heads[group] * mics, jnp.where(which == halves + 1, heads[group], 0.0))
            starts[group, b] = jnp.sum(jnp.where(mine, number, 0.0)).astype(jnp.int32)

    def one_source(i, after):
        source = sources - 1 - i
        before = []
        for group in range(groups):
            x = moved_ref[source * groups + group].astype(f32)
            first = pl.multiple_of(source * mics, mics)
            wide_ref[group, pl.ds(first, mics - 8), :] = x[: mics - 8]
            wide_ref[group, pl.ds(first + mics - 8, 8), :] = x[mics - 8 :] + jnp.where(row8 == 7, after[group], 0.0)
            before.append(carried(x))
        return tuple(before)

    lax.fori_loop(0, sources, one_source, tuple(carried(x) for x in heads), unroll=32)
    for group in range(groups):
        wide_ref[group, total : total + PIECE, :] = wide_ref[group, 0:PIECE, :]

    depth = total // chunks
    for piece in range(total // PIECE):
        for group in range(groups):
            begin = [(starts[group, b] + piece * PIECE) % total for b in range(blocks)]
            rows = [wide_ref[group, pl.ds(s, PIECE), :] for s in begin]
            mixed = jnp.where(of_block == 0, rows[0], rows[1]).astype(bf16)
            rows_ref[piece * PIECE : (piece + 1) * PIECE, group * LANES : (group + 1) * LANES] = mixed
        end = (piece + 1) * PIECE
        if end % depth == 0:
            chunk = end // depth - 1
            copies[chunk].wait()
            product = jnp.dot(steer_ref[chunk], rows_ref[end - depth : end, :], preferred_element_type=f32)
            if chunk == 0:
                sum_ref[...] = product
            else:
                sum_ref[...] += product

    points = out_ref.shape[1]
    slot = blocks * halves
    imaginary = lane // slot % 2 == 1
    for j in range(out_ref.shape[0]):
        power = jnp.zeros((points, LANES), f32)
        for group in range(groups):
            cols = slice(group * LANES, (group + 1) * LANES)
            by_cos = sum_ref[2 * j * points : (2 * j + 1) * points, cols]
            by_sin = sum_ref[(2 * j + 1) * points : (2 * j + 2) * points, cols]
            other = jnp.where(imaginary, -pltpu.roll(by_sin, slot, 1), pltpu.roll(by_sin, LANES - slot, 1))
            both = by_cos + other
            power = power + both * both
        power = jnp.where(~spare & (lane // (2 * slot) == j), power, 0.0)
        out_ref[j : j + 1, :] = jnp.sum(power.T, 0, keepdims=True) * scale


def beam(moved, steer, mics, blocks, halves, groups, points, scale):
    total = moved.shape[0] // groups * mics
    chunks, rows, depth = steer.shape
    bins = rows // (2 * points)
    body = lambda *refs: beam_body(*refs, mics=mics, blocks=blocks, halves=halves, groups=groups, scale=scale)
    vmem = pl.BlockSpec(memory_space=pltpu.VMEM)
    return pl.pallas_call(
        body,
        out_shape=jax.ShapeDtypeStruct((bins, points), f32),
        in_specs=[vmem, pl.BlockSpec(memory_space=pltpu.HBM)],
        out_specs=vmem,
        scratch_shapes=[
            pltpu.VMEM((groups, total + PIECE, LANES), f32),
            pltpu.VMEM((total, groups * LANES), bf16),
            pltpu.VMEM((rows, groups * LANES), f32),
            pltpu.VMEM(steer.shape, bf16),
            pltpu.SemaphoreType.DMA((chunks,)),
        ],
        name="beam",
    )(moved, steer)


def local(signal, offsets, fraction, radius, azimuth):
    blocks, mics, length = signal.shape
    sectors, groups = lax.axis_size("sector"), lax.axis_size("blk")
    owners = sectors * groups
    halves = length // HALF
    bins = HALF // owners
    spectra = local_spectra(signal, offsets, fraction, owners)
    moved = lax.all_to_all(spectra, ("sector", "blk"), split_axis=0, concat_axis=0, tiled=True)
    moved = pltpu.with_memory_space_constraint(moved, pltpu.VMEM)
    first = (lax.axis_index("sector") * groups + lax.axis_index("blk")) * bins
    total_mics = sectors * mics
    steer = steering(first, bins, radius, azimuth, total_mics)
    scale = 1.0 / (total_mics * blocks * (halves - 1) * groups)
    return beam(moved, steer, mics, blocks, halves, groups, radius.shape[0], scale)


def solution(mesh):
    return jax.shard_map(
        local,
        mesh=mesh,
        in_specs=(P("blk", "sector", None), P("blk"), P("blk", None), P(), P()),
        out_specs=P(("sector", "blk"), None),
        check_vma=False,
    )
```

time: 84.9 us -> 84.7 us (level)
  Pallas kernels: 39.4 us -> 34.7 us
  waiting for transfers between devices: 25.9 us -> 30.4 us
    all_to_all x1, waiting for transfers between devices: 25.9 us -> 30.4 us  [local(): lax.all_to_all(spectra, ('sector', 'blk'), split_axis=0, concat_axis=0, t...]
    pallas_call x1, Pallas kernels: 24.6 us -> 20 us  [steering(): pl.pallas_call(steer_body, grid=(total_mics // STEER_COLS,), out_shape=ja...]
  transfers between devices with their start and end apart: 1 -> 1, of which waited for: 1 -> 1; matrix products, arithmetic and copies ran while one was open for 4% -> 4% of each run, Pallas kernels for 29% -> 24%
where the time goes in v4:
time: 84.7 us; the launch traced here: 84.4 us
  Pallas kernels  34.7 us (41%)
  waiting for transfers between devices  30.4 us (36%)
  starting transfers between devices  15.7 us (19%)
  local copies, waits for them, and re-layouts  2.4 us (3%)
  other arithmetic  1.15 us (1%)
    all_to_all x1, waiting for transfers between devices, local(): lax.all_to_all(spectra, ('sector', 'blk'), split_axis=0, concat_axis=0, t...  30.4 us
    pallas_call x1, Pallas kernels, steering(): pl.pallas_call(steer_body, grid=(total_mics // STEER_COLS,), out_shape=ja...  20 us
    all_to_all x1, starting transfers between devices, local(): lax.all_to_all(spectra, ('sector', 'blk'), split_axis=0, concat_axis=0, t...  15.7 us
    pallas_call x1, Pallas kernels, beam(): pl.pallas_call(body, out_shape=jax.ShapeDtypeStruct((bins, points), f32),...  7.57 us
    pallas_call x1, Pallas kernels, local_spectra(): pl.pallas_call(spectra_body, out_shape=jax.ShapeDtypeStruct((owners, mics...  7.14 us
  transfers between devices with their start and end apart: 1, of which 1 were waited for; matrix products, arithmetic and copies ran while one was open for 4% of the time, Pallas kernels for 24%

profile of v4, /device:TPU:1, one launch (start us, length us, event | category | flops | bytes accessed | tf_op | source)
XLA Modules:
  0.0 84.4 jit_solution(10913662477199363268)
XLA Ops:
  0.0 7.1 %spectra.1 = bf16[256,32,128]{2,1,0:T(8,128)(2,1)} custom-call(s32[2]{0:T(128)} %offsets_ref.1, bf16[2,32,8192]{2,1,0:T(8,128)(2,1)} %signal_hbm.1, f32[2,8192]{1,0:T(2,128)} %fraction_hbm.1, bf16[4,1024,256]{2,1,0:T(8,128)(2,1)} %constant.16.clone.table_hbm), custom_call_target="tpu_custom_call" | custom-call | tf_op jit(solution)/shard_map/spectra/pallas_call | solution.py:134
  7.1 0.0 copy-start
  7.2 0.0 copy-start.1
  7.2 15.7 %all-to-all-start = ((bf16[256,32,128]{2,1,0:T(8,128)(2,1)}), bf16[256,32,128]{2,1,0:T(8,128)(2,1)S(1)}, u32[]{:S(2)}, u32[]{:S(2)}) async-start(bf16[256,32,128]{2,1,0:T(8,128)(2,1)} %spectra.1), calls=%async_computation | async-start | bytes 4194304 | tf_op jit(solution)/shard_map/all_to_all | solution.py:324
  22.8 0.0 copy-done
  22.8 0.0 copy-done.1
  22.9 0.8 copy.8.across_ref
  23.7 0.8 copy.9.along_ref
  24.5 0.8 copy.7.base_ref
  25.3 0.5 fusion
  25.8 0.6 pad_maximum_fusion.cycle_ref
  26.4 20.0 %steer.1.refs_1_ = bf16[4,1024,1024]{2,1,0:T(8,128)(2,1)} custom-call(s32[1]{0:T(128)} %bitcast.first_ref, f32[2,4096]{1,0:T(2,128)} %pad_maximum_fusion.cycle_ref, f32[256,1]{1,0:T(8,128)} %copy.7.base_ref, f32[256,1]{1,0:T(8,128)} %copy.8.across_ref, f32[256,1]{1,0:T(8,128)} %copy.9.along_ref), custom_call_target="tpu_custom_call" | custom-call | tf_op jit(solution)/shard_map/steer/pallas_call | solution.py:202
  46.4 30.4 %all-to-all-done.refs_0_ = bf16[256,32,128]{2,1,0:T(8,128)(2,1)S(1)} async-done(((bf16[256,32,128]{2,1,0:T(8,128)(2,1)}), bf16[256,32,128]{2,1,0:T(8,128)(2,1)S(1)}, u32[]{:S(2)}, u32[]{:S(2)}) %all-to-all-start) | async-done | bytes 2097184 | tf_op jit(solution)/shard_map/all_to_all | solution.py:324
  76.9 7.6 %beam.1 = f32[2,256]{1,0:T(2,128)} custom-call(bf16[256,32,128]{2,1,0:T(8,128)(2,1)S(1)} %all-to-all-done.refs_0_, bf16[4,1024,1024]{2,1,0:T(8,128)(2,1)} %steer.1.refs_1_), custom_call_target="tpu_custom_call" | custom-call | tf_op jit(solution)/shard_map/beam/pallas_call | solution.py:301
  (1 shorter events, 0.0 us)
Async XLA Ops:
  7.1 15.7 %copy-start = (f32[256]{0:T(256)S(1)}, f32[256]{0:T(256)}, u32[]{:S(2)}) copy-start(f32[256]{0:T(256)} %param.9) | copy-start | bytes 3076
  7.2 15.7 %copy-start.1 = (f32[256]{0:T(256)S(1)}, f32[256]{0:T(256)}, u32[]{:S(2)}) copy-start(f32[256]{0:T(256)} %param.10) | copy-start | bytes 3076
  7.2 69.7 %all-to-all-start = ((bf16[256,32,128]{2,1,0:T(8,128)(2,1)}), bf16[256,32,128]{2,1,0:T(8,128)(2,1)S(1)}, u32[]{:S(2)}, u32[]{:S(2)}) async-start(bf16[256,32,128]{2,1,0:T(8,128)(2,1)} %spectra.1), calls=%async_computation | async-start | bytes 4194304 | tf_op jit(solution)/shard_map/all_to_all | solution.py:324
